TPU v7x, 256 devices: a whole 4x4x8 slice. The times are simulated.
256 devices in a mesh: gx: 8 (over y_lo, x), gy: 32 (over z, y_hi, core).
Axes of the slice: x: 4, y: 4 (y_hi: 2, y_lo: 2; y = y_hi * 2 + y_lo), z: 8, core: 2. Of those that a mesh axis runs over, the one named last changes fastest.
Arguments:
- adjoint_source: float32 [2, 128, 256, 128], P(None, 'gx', 'gy'), may hold values from -16 to 16
- storage: float32 [4, 128, 256, 128], P(None, 'gx', 'gy'), may hold values from -0.2 to 2, as said below
- soil_ids: int32 [128, 256, 128], P('gx', 'gy'), may hold values from 0 to 15
- bc_mask: int32 [128, 256], P('gx', 'gy'), may hold values 0 or 1
- soil_props: float32 [3, 16], replicated, may hold values from 0.1 to 1
Outputs:
- adjoint: float32 [2, 128, 256, 128], P(None, 'gx', 'gy')
- residual: float32 [2, 128, 256, 128], P(None, 'gx', 'gy')
- next_basis: float32 [2, 128, 256, 128], P(None, 'gx', 'gy')
Inputs may be any that keep to these rules, and one draw needn't show every extreme that they name: `storage`: sp and St lie in 0.2 to 2, Spt within -0.04 to 0.04, Stp within -0.2 to 0.2.
All inputs are finite; a program needn't handle non-finite values. No bound on the sum of `bc_mask` on one device may be relied on, other than what follows from the above.
Results may differ from a plain program's by a relative error of at most 0.0008.
Values sent between devices are 32-bit elements; how exact they have to be, the bound alone decides.
A program may use at most 64 MiB of HBM per device.

v0:
```python
import math

import jax
import jax.numpy as jnp
from jax import lax
from jax.sharding import PartitionSpec as P

NMAT = 16
MARGIN = 4
SWEEPS = 6
ITERS = 2


epsilon = 1e-06


def padded_2(block, sides, width):
    for axis, dim in sides:
        count = lax.axis_size(axis)
        forward = [(i, i + 1) for i in range(count - 1)]
        backward = [(target, source) for source, target in forward]
        low = lax.ppermute(
            lax.slice_in_dim(block, block.shape[dim] - width, None, axis=dim), axis, forward
        )
        high = lax.ppermute(lax.slice_in_dim(block, 0, width, axis=dim), axis, backward)
        block = jnp.concatenate([low, block, high], axis=dim)
    return block


def neighbour_list(field):
    middle = field[1:-1, 1:-1]
    below = jnp.pad(middle[:, :, :-1], ((0, 0), (0, 0), (1, 0)))
    above = jnp.pad(middle[:, :, 1:], ((0, 0), (0, 0), (0, 1)))
    return [field[:-2, 1:-1], field[2:, 1:-1], field[1:-1, :-2], field[1:-1, 2:], below, above]


def face_parts(coefficients):
    centre = coefficients[:, 1:-1, 1:-1]
    press_faces = jnp.stack(
        [jnp.sqrt(centre[0] * other) for other in neighbour_list(coefficients[0])]
    )
    heat_faces = jnp.stack(
        [jnp.sqrt(centre[1] * other) for other in neighbour_list(coefficients[1])]
    )
    return (press_faces, heat_faces, centre)


def laplace(field, faces, diagonal):
    total = diagonal * field[1:-1, 1:-1]
    for index, other in enumerate(neighbour_list(field)):
        total = total - faces[index] * other
    return total


def apply_adjoint(padded, spread_e, press_faces, heat_faces, centre):
    press_part = padded[0]
    heat_part = padded[1]
    mixed = press_part + spread_e * heat_part
    press_diag = jnp.sum(press_faces, axis=0) + centre[7]
    heat_diag = jnp.sum(heat_faces, axis=0)
    press_mid = press_part[1:-1, 1:-1]
    heat_mid = heat_part[1:-1, 1:-1]
    press_out = (
        centre[3] * press_mid + laplace(mixed, press_faces, press_diag) + centre[5] * heat_mid
    )
    heat_out = (
        centre[4] * press_mid + centre[6] * heat_mid + laplace(heat_part, heat_faces, heat_diag)
    )
    return jnp.stack([press_out, heat_out])


def block_inverse(press_faces, heat_faces, centre, outside):
    press_diag = jnp.sum(press_faces, axis=0) + centre[7]
    heat_diag = jnp.sum(heat_faces, axis=0)
    first = centre[3] + press_diag + outside
    cross = centre[5] + centre[2] * press_diag
    lower = centre[4]
    last = centre[6] + heat_diag + outside
    determinant = first * last - cross * lower
    return (last / determinant, -cross / determinant, -lower / determinant, first / determinant)


def subdomain_solve(rhs, press_faces, heat_faces, centre, inverse, spread_e):
    solution = jnp.zeros_like(rhs)
    for sweep in range(SWEEPS):
        padded = jnp.pad(solution, ((0, 0), (1, 1), (1, 1), (0, 0)))
        remain = rhs - apply_adjoint(padded, spread_e, press_faces, heat_faces, centre)
        step_p = inverse[0] * remain[0] + inverse[1] * remain[1]
        step_t = inverse[2] * remain[0] + inverse[3] * remain[1]
        solution = solution + jnp.stack([step_p, step_t])
    return solution


def assemble(material, storage, bc_mask):
    depth = material.shape[3]
    top = lax.broadcasted_iota(jnp.int32, (1, 1, depth), 2) == depth - 1
    boundary = jnp.where(top, 2.0 * material[0] * bc_mask[:, :, None].astype(jnp.float32), 0.0)
    return jnp.concatenate([material, storage, boundary[None]], axis=0)


def lookup(soil_props, ident):
    levels = jnp.arange(NMAT, dtype=jnp.float32)[:, None, None, None]
    onehot = (ident[None] == levels).astype(jnp.float32)
    return jnp.einsum("km,mxyz->kxyz", soil_props, onehot, precision=lax.Precision.HIGHEST)


def least_squares(columns, beta):
    count = len(columns)
    target = [beta] + [0.0 * beta for index in range(count)]
    rotations = []
    upper = []
    for column_index, column in enumerate(columns):
        values = list(column)
        for index, pair in enumerate(rotations):
            high = pair[0] * values[index] + pair[1] * values[index + 1]
            low = -pair[1] * values[index] + pair[0] * values[index + 1]
            values[index] = high
            values[index + 1] = low
        radius = jnp.sqrt(
            values[column_index] * values[column_index]
            + values[column_index + 1] * values[column_index + 1]
        )
        cosine = values[column_index] / radius
        sine = values[column_index + 1] / radius
        values[column_index] = radius
        rotations.append((cosine, sine))
        high = cosine * target[column_index] + sine * target[column_index + 1]
        low = -sine * target[column_index] + cosine * target[column_index + 1]
        target[column_index] = high
        target[column_index + 1] = low
        upper.append(values[: column_index + 1])
    weights = [None] * count
    for index in reversed(range(count)):
        accum = target[index]
        for later in range(index + 1, count):
            accum = accum - upper[later][index] * weights[later]
        weights[index] = accum / upper[index][index]
    return weights


def fold_axis(padded, count, axis):
    width = MARGIN
    total = lax.slice_in_dim(padded, 2 * width, 2 * width + count, axis=axis)
    lower = lax.slice_in_dim(padded, 0, width, axis=axis)
    upper = lax.slice_in_dim(padded, count + 3 * width, count + 4 * width, axis=axis)
    spread_low = [(0, 0)] * padded.ndim
    spread_low[axis] = (0, count - width)
    spread_high = [(0, 0)] * padded.ndim
    spread_high[axis] = (count - width, 0)
    return total + jnp.pad(lower, spread_low) + jnp.pad(upper, spread_high)


def global_length(vector):
    return jnp.sqrt(lax.psum(jnp.sum(vector * vector), ("gx", "gy")) + epsilon)


def shards(adjoint_source, storage, soil_ids, bc_mask, soil_props):
    rows_x = soil_ids.shape[0]
    rows_y = soil_ids.shape[1]
    depth = soil_ids.shape[2]
    cycle = MARGIN + 1
    material = lookup(soil_props, soil_ids.astype(jnp.float32))
    fields = assemble(material, storage, bc_mask)
    widened = padded_2(fields, (("gx", 1), ("gy", 2)), cycle)
    start_x = lax.axis_index("gx") * rows_x - MARGIN
    start_y = lax.axis_index("gy") * rows_y - MARGIN
    along_x = start_x + jnp.arange(rows_x + 2 * MARGIN, dtype=jnp.int32)
    along_y = start_y + jnp.arange(rows_y + 2 * MARGIN, dtype=jnp.int32)
    inside_x = (along_x >= 0) & (along_x < rows_x * lax.axis_size("gx"))
    inside_y = (along_y >= 0) & (along_y < rows_y * lax.axis_size("gy"))
    outside = (1.0 - (inside_x[:, None] & inside_y[None, :]).astype(jnp.float32))[:, :, None]
    sub_press, sub_heat, sub_centre = face_parts(widened)
    sub_inverse = block_inverse(sub_press, sub_heat, sub_centre, outside)
    own_coeffs = widened[:, MARGIN:-MARGIN, MARGIN:-MARGIN]
    own_press, own_heat, own_centre = face_parts(own_coeffs)
    beta = global_length(adjoint_source)
    basis = [adjoint_source / beta]
    directions = []
    columns = []
    for column_index in range(ITERS):
        rhs = jnp.pad(basis[-1], ((0, 0), (MARGIN, MARGIN), (MARGIN, MARGIN), (0, 0)))
        solved = subdomain_solve(rhs, sub_press, sub_heat, sub_centre, sub_inverse, widened[2])
        gathered = padded_2(solved, (("gx", 1), ("gy", 2)), MARGIN)
        direction = fold_axis(fold_axis(gathered, rows_x, 1), rows_y, 2)
        directions.append(direction)
        padded = padded_2(direction, (("gx", 1), ("gy", 2)), 1)
        image = apply_adjoint(padded, own_coeffs[2], own_press, own_heat, own_centre)
        heights = []
        for prior in basis:
            height = lax.psum(jnp.sum(image * prior), ("gx", "gy"))
            image = image - height * prior
            heights.append(height)
        length = global_length(image)
        heights.append(length)
        columns.append(heights)
        basis.append(image / length)
    weights = least_squares(columns, beta)
    adjoint = weights[0] * directions[0]
    adjoint = adjoint + weights[1] * directions[1]
    residual = jnp.zeros_like(adjoint_source)
    for row in range(ITERS + 1):
        factor = beta if row == 0 else 0.0 * beta
        for column_index in range(ITERS):
            if row <= column_index + 1:
                factor = factor - columns[column_index][row] * weights[column_index]
        residual = residual + factor * basis[row]
    cell_count = 2.0 * rows_x * lax.axis_size("gx") * rows_y * lax.axis_size("gy") * depth
    next_basis = basis[-1] * math.sqrt(cell_count)
    return (adjoint, residual, next_basis)


def solution(mesh):
    in_specs = (
        P(None, "gx", "gy", None),
        P(None, "gx", "gy", None),
        P("gx", "gy", None),
        P("gx", "gy"),
        P(),
    )
    out_specs = (P(None, "gx", "gy", None), P(None, "gx", "gy", None), P(None, "gx", "gy", None))
    return jax.shard_map(shards, mesh=mesh, in_specs=in_specs, out_specs=out_specs, check_vma=False)
```

profile of v0, /device:TPU:1, one launch (start us, length us, event | category | flops | bytes accessed | tf_op | source)
XLA Modules:
  0.0 611.9 jit_solution(17530012090384040038)
XLA Ops:
  5.2 4.6 collective-permute-start
  9.8 1.5 multiply_reduce_fusion.5
  11.9 81.7 %psum.42 = f32[]{:T(128)} all-reduce(f32[]{:T(128)} %multiply_reduce_fusion.5), channel_id=1, replica_groups=mesh['gx'=8,'gy'=32] {'gx','gy'}, use_global_device_ids=true, to_apply=%region_1.2 | all-reduce | flops 1 | bytes 8 | tf_op jit(solution)/shard_map/psum | solution.py:154
  95.9 2.7 collective-permute-start.3
  98.8 4.5 collective-permute-start.2
  103.4 4.7 collective-permute-done.3
  108.3 4.3 collective-permute-done.2
  124.2 4.0 collective-permute-start.4
  128.2 1.3 collective-permute-done.4
  129.6 1.9 collective-permute-start.7
  131.5 7.2 %collective-permute-start.6 = (f32[2,32,4,128]{3,2,1,0:T(4,128)S(1)}, f32[2,32,4,128]{3,2,1,0:T(4,128)S(1)}, u32[]{:S(2)}, u32[]{:S(2)}) collective-permute-start(f32[2,32,4,128]{3,2,1,0:T(4,128)S(1)} %get-tuple-element.37), channel_id=1, source_target_pairs={{0,1},{1,2},{2,3},{3,4},{4,5},{5,6},{6,7},{7,8},{8,9},{9,10},{10,1... | collective-permute-start | bytes 393224 | tf_op jit(solution)/shard_map/ppermute | solution.py:22
  142.2 4.6 collective-permute-start.8
  147.6 1.9 collective-permute-start.11
  149.5 6.7 %collective-permute-start.10 = (f32[2,18,1,128]{3,2,1,0:T(1,128)S(1)}, f32[2,18,1,128]{3,2,1,0:T(1,128)S(1)}, u32[]{:S(2)}, u32[]{:S(2)}) collective-permute-start(f32[2,18,1,128]{3,2,1,0:T(1,128)S(1)} %get-tuple-element.153), channel_id=1, source_target_pairs={{0,1},{1,2},{2,3},{3,4},{4,5},{5,6},{6,7},{7,8},{8,9},{9,10},{10,1... | collective-permute-start | bytes 55304 | tf_op jit(solution)/shard_map/ppermute | solution.py:22
  160.4 83.1 %psum.43 = f32[]{:T(128)} all-reduce(f32[]{:T(128)} %multiply_reduce_fusion.4), channel_id=1, replica_groups=mesh['gx'=8,'gy'=32] {'gx','gy'}, use_global_device_ids=true, to_apply=%region_3.4 | all-reduce | flops 1 | bytes 8 | tf_op jit(solution)/shard_map/psum | solution.py:190
  243.5 2.3 multiply_reduce_fusion.3
  245.8 74.8 %psum.44 = f32[]{:T(128)} all-reduce(f32[]{:T(128)} %multiply_reduce_fusion.3), channel_id=1, replica_groups=mesh['gx'=8,'gy'=32] {'gx','gy'}, use_global_device_ids=true, to_apply=%region_5.6 | all-reduce | flops 1 | bytes 8 | tf_op jit(solution)/shard_map/psum | solution.py:154
  321.2 1.7 broadcast_divide_fusion.1
  334.8 4.0 collective-permute-start.12
  338.8 1.3 collective-permute-done.12
  340.1 3.7 collective-permute-start.15
  343.9 3.5 collective-permute-start.14
  347.9 1.4 collective-permute-done.14
  351.1 4.4 collective-permute-start.16
  356.3 1.9 collective-permute-start.19
  358.3 6.7 %collective-permute-start.18 = (f32[2,18,1,128]{3,2,1,0:T(1,128)S(1)}, f32[2,18,1,128]{3,2,1,0:T(1,128)S(1)}, u32[]{:S(2)}, u32[]{:S(2)}) collective-permute-start(f32[2,18,1,128]{3,2,1,0:T(1,128)S(1)} %get-tuple-element.143), channel_id=1, source_target_pairs={{0,1},{1,2},{2,3},{3,4},{4,5},{5,6},{6,7},{7,8},{8,9},{9,10},{10,1... | collective-permute-start | bytes 55304 | tf_op jit(solution)/shard_map/ppermute | solution.py:22
  369.6 82.6 %psum.45 = f32[]{:T(128)} all-reduce(f32[]{:T(128)} %multiply_reduce_fusion.2), channel_id=1, replica_groups=mesh['gx'=8,'gy'=32] {'gx','gy'}, use_global_device_ids=true, to_apply=%region_7.8 | all-reduce | flops 1 | bytes 8 | tf_op jit(solution)/shard_map/psum | solution.py:190
  452.8 1.9 multiply_reduce_fusion.1
  454.7 73.7 %psum.46 = f32[]{:T(128)} all-reduce(f32[]{:T(128)} %get-tuple-element.3), channel_id=1, replica_groups=mesh['gx'=8,'gy'=32] {'gx','gy'}, use_global_device_ids=true, to_apply=%region_9.10 | all-reduce | flops 1 | bytes 8 | tf_op jit(solution)/shard_map/psum | solution.py:190
  529.0 2.0 multiply_reduce_fusion
  531.0 74.0 %psum.47 = f32[]{:T(128)} all-reduce(f32[]{:T(128)} %multiply_reduce_fusion), channel_id=1, replica_groups=mesh['gx'=8,'gy'=32] {'gx','gy'}, use_global_device_ids=true, to_apply=%region_11.12 | all-reduce | flops 1 | bytes 8 | tf_op jit(solution)/shard_map/psum | solution.py:154
  609.8 2.1 broadcast_multiply_fusion
  (314 shorter events, 43.9 us)
Async XLA Ops:
  2.0 110.8 %copy-start.27 = (f32[3,16,8,128]{3,2,1,0:T(8,128)}, f32[3,16,8,128]{3,2,1,0:T(8,128)S(1)}, u32[]{:S(2)}) copy-start(f32[3,16,8,128]{3,2,1,0:T(8,128)S(1)} %copy.14) | copy-start | bytes 589828
  2.9 109.9 %copy-start.41 = (f32[1,16,8,128]{3,2,1,0:T(8,128)}, f32[1,16,8,128]{3,2,1,0:T(8,128)S(1)}, u32[]{:S(2)}) copy-start(f32[1,16,8,128]{3,2,1,0:T(8,128)S(1)} %multiply_select_fusion) | copy-start | bytes 196612
  3.9 90.6 %collective-permute-start.1 = (f32[8,5,8,128]{3,2,1,0:T(8,128)S(1)}, f32[8,5,8,128]{3,2,1,0:T(8,128)S(1)}, u32[]{:S(2)}, u32[]{:S(2)}) collective-permute-start(f32[8,5,8,128]{3,2,1,0:T(8,128)S(1)} %get-tuple-element.40), channel_id=1, source_target_pairs={{32,0},{64,32},{96,64},{128,96},{160,128},{192,160},{224,192},{33,... | collective-permute-start | bytes 491528 | tf_op jit(solution)/shard_map/ppermute | solution.py:25
  5.2 89.3 %collective-permute-start = (f32[8,5,8,128]{3,2,1,0:T(8,128)S(1)}, f32[8,5,8,128]{3,2,1,0:T(8,128)S(1)}, u32[]{:S(2)}, u32[]{:S(2)}) collective-permute-start(f32[8,5,8,128]{3,2,1,0:T(8,128)S(1)} %get-tuple-element.39), channel_id=1, source_target_pairs={{0,32},{32,64},{64,96},{96,128},{128,160},{160,192},{192,224},{1,3... | collective-permute-start | bytes 491528 | tf_op jit(solution)/shard_map/ppermute | solution.py:22
  94.4 18.4 %copy-start.37 = (f32[8,5,8,128]{3,2,1,0:T(8,128)}, f32[8,5,8,128]{3,2,1,0:T(8,128)S(1)}, u32[]{:S(2)}) copy-start(f32[8,5,8,128]{3,2,1,0:T(8,128)S(1)} %collective-permute-done.1) | copy-start | bytes 491524
  94.5 18.4 %copy-start.39 = (f32[8,5,8,128]{3,2,1,0:T(8,128)}, f32[8,5,8,128]{3,2,1,0:T(8,128)S(1)}, u32[]{:S(2)}) copy-start(f32[8,5,8,128]{3,2,1,0:T(8,128)S(1)} %collective-permute-done) | copy-start | bytes 491524
  95.9 12.2 %collective-permute-start.3 = (f32[8,26,5,128]{3,0,2,1:T(8,128)S(1)}, f32[8,26,5,128]{3,0,2,1:T(8,128)S(1)}, u32[]{:S(2)}, u32[]{:S(2)}) collective-permute-start(f32[8,26,5,128]{3,0,2,1:T(8,128)S(1)} %copy.16), channel_id=1, source_target_pairs={{1,0},{2,1},{3,2},{4,3},{5,4},{6,5},{7,6},{8,7},{9,8},{10,9},{11,1... | collective-permute-start | bytes 1597448 | tf_op jit(solution)/shard_map/ppermute | solution.py:25
  98.8 13.8 %collective-permute-start.2 = (f32[8,26,5,128]{3,0,2,1:T(8,128)S(1)}, f32[8,26,5,128]{3,0,2,1:T(8,128)S(1)}, u32[]{:S(2)}, u32[]{:S(2)}) collective-permute-start(f32[8,26,5,128]{3,0,2,1:T(8,128)S(1)} %copy.15), channel_id=1, source_target_pairs={{0,1},{1,2},{2,3},{3,4},{4,5},{5,6},{6,7},{7,8},{8,9},{9,10},{10,1... | collective-permute-start | bytes 1597448 | tf_op jit(solution)/shard_map/ppermute | solution.py:22
  122.9 5.3 collective-permute-start.5
  124.2 5.3 collective-permute-start.4
  129.6 10.3 %collective-permute-start.7 = (f32[2,32,4,128]{3,2,1,0:T(4,128)S(1)}, f32[2,32,4,128]{3,2,1,0:T(4,128)S(1)}, u32[]{:S(2)}, u32[]{:S(2)}) collective-permute-start(f32[2,32,4,128]{3,2,1,0:T(4,128)S(1)} %get-tuple-element.38), channel_id=1, source_target_pairs={{1,0},{2,1},{3,2},{4,3},{5,4},{6,5},{7,6},{8,7},{9,8},{10,9},{11,1... | collective-permute-start | bytes 393224 | tf_op jit(solution)/shard_map/ppermute | solution.py:25
  131.5 9.0 %collective-permute-start.6 = (f32[2,32,4,128]{3,2,1,0:T(4,128)S(1)}, f32[2,32,4,128]{3,2,1,0:T(4,128)S(1)}, u32[]{:S(2)}, u32[]{:S(2)}) collective-permute-start(f32[2,32,4,128]{3,2,1,0:T(4,128)S(1)} %get-tuple-element.37), channel_id=1, source_target_pairs={{0,1},{1,2},{2,3},{3,4},{4,5},{5,6},{6,7},{7,8},{8,9},{9,10},{10,1... | collective-permute-start | bytes 393224 | tf_op jit(solution)/shard_map/ppermute | solution.py:22
  139.8 18.6 %copy-start.49 = (f32[1,16,8,128]{3,0,2,1:T(1,128)}, f32[1,16,8,128]{3,0,2,1:T(1,128)S(1)}, u32[]{:S(2)}) copy-start(f32[1,16,8,128]{3,0,2,1:T(1,128)S(1)} %slice.1689) | copy-start | bytes 196612
  139.9 18.2 %copy-start.29 = (f32[18,10,128]{2,1,0:T(8,128)}, f32[18,10,128]{2,1,0:T(8,128)S(1)}, u32[]{:S(2)}) copy-start(f32[18,10,128]{2,1,0:T(8,128)S(1)} %get-tuple-element.29) | copy-start | bytes 276484
  139.9 18.5 %copy-start.31 = (f32[18,10,128]{2,1,0:T(8,128)}, f32[18,10,128]{2,1,0:T(8,128)S(1)}, u32[]{:S(2)}) copy-start(f32[18,10,128]{2,1,0:T(8,128)S(1)} %get-tuple-element.30) | copy-start | bytes 276484
  140.9 6.0 collective-permute-start.9
  142.2 5.4 collective-permute-start.8
  147.6 8.8 %collective-permute-start.11 = (f32[2,18,1,128]{3,2,1,0:T(1,128)S(1)}, f32[2,18,1,128]{3,2,1,0:T(1,128)S(1)}, u32[]{:S(2)}, u32[]{:S(2)}) collective-permute-start(f32[2,18,1,128]{3,2,1,0:T(1,128)S(1)} %get-tuple-element.154), channel_id=1, source_target_pairs={{1,0},{2,1},{3,2},{4,3},{5,4},{6,5},{7,6},{8,7},{9,8},{10,9},{11,1... | collective-permute-start | bytes 55304 | tf_op jit(solution)/shard_map/ppermute | solution.py:25
  149.5 7.6 %collective-permute-start.10 = (f32[2,18,1,128]{3,2,1,0:T(1,128)S(1)}, f32[2,18,1,128]{3,2,1,0:T(1,128)S(1)}, u32[]{:S(2)}, u32[]{:S(2)}) collective-permute-start(f32[2,18,1,128]{3,2,1,0:T(1,128)S(1)} %get-tuple-element.153), channel_id=1, source_target_pairs={{0,1},{1,2},{2,3},{3,4},{4,5},{5,6},{6,7},{7,8},{8,9},{9,10},{10,1... | collective-permute-start | bytes 55304 | tf_op jit(solution)/shard_map/ppermute | solution.py:22
  333.5 5.3 collective-permute-start.13
  334.8 5.3 collective-permute-start.12
  340.1 7.8 %collective-permute-start.15 = (f32[2,32,4,128]{3,2,1,0:T(4,128)S(1)}, f32[2,32,4,128]{3,2,1,0:T(4,128)S(1)}, u32[]{:S(2)}, u32[]{:S(2)}) collective-permute-start(f32[2,32,4,128]{3,2,1,0:T(4,128)S(1)} %get-tuple-element.36), channel_id=1, source_target_pairs={{1,0},{2,1},{3,2},{4,3},{5,4},{6,5},{7,6},{8,7},{9,8},{10,9},{11,1... | collective-permute-start | bytes 393224 | tf_op jit(solution)/shard_map/ppermute | solution.py:25
  343.8 23.5 %copy-start.48 = (f32[18,10,128]{2,1,0:T(8,128)S(1)}, f32[18,10,128]{2,1,0:T(8,128)}, u32[]{:S(2)}) copy-start(f32[18,10,128]{2,1,0:T(8,128)} %get-tuple-element.6) | copy-start | bytes 276484
  343.9 5.4 collective-permute-start.14
  349.7 19.2 %copy-start.26 = (f32[2,16,8,128]{3,2,1,0:T(8,128)S(1)}, f32[2,16,8,128]{3,2,1,0:T(8,128)}, u32[]{:S(2)}) copy-start(f32[2,16,8,128]{3,2,1,0:T(8,128)} %param.5) | copy-start | bytes 393220
  349.8 5.8 collective-permute-start.17
  351.1 101.7 %copy-start.34 = (f32[1,16,8,128]{3,2,1,0:T(8,128)S(1)}, f32[1,16,8,128]{3,2,1,0:T(8,128)}, u32[]{:S(2)}) copy-start(f32[1,16,8,128]{3,2,1,0:T(8,128)} %copy-done.33) | copy-start | bytes 196612
  351.1 101.7 %copy-start.36 = (f32[1,16,8,128]{3,2,1,0:T(8,128)S(1)}, f32[1,16,8,128]{3,2,1,0:T(8,128)}, u32[]{:S(2)}) copy-start(f32[1,16,8,128]{3,2,1,0:T(8,128)} %copy-done.35) | copy-start | bytes 196612
  351.1 5.2 collective-permute-start.16
  356.3 10.8 %collective-permute-start.19 = (f32[2,18,1,128]{3,2,1,0:T(1,128)S(1)}, f32[2,18,1,128]{3,2,1,0:T(1,128)S(1)}, u32[]{:S(2)}, u32[]{:S(2)}) collective-permute-start(f32[2,18,1,128]{3,2,1,0:T(1,128)S(1)} %get-tuple-element.144), channel_id=1, source_target_pairs={{1,0},{2,1},{3,2},{4,3},{5,4},{6,5},{7,6},{8,7},{9,8},{10,9},{11,1... | collective-permute-start | bytes 55304 | tf_op jit(solution)/shard_map/ppermute | solution.py:25
  358.3 8.9 %collective-permute-start.18 = (f32[2,18,1,128]{3,2,1,0:T(1,128)S(1)}, f32[2,18,1,128]{3,2,1,0:T(1,128)S(1)}, u32[]{:S(2)}, u32[]{:S(2)}) collective-permute-start(f32[2,18,1,128]{3,2,1,0:T(1,128)S(1)} %get-tuple-element.143), channel_id=1, source_target_pairs={{0,1},{1,2},{2,3},{3,4},{4,5},{5,6},{6,7},{7,8},{8,9},{9,10},{10,1... | collective-permute-start | bytes 55304 | tf_op jit(solution)/shard_map/ppermute | solution.py:22
  367.2 240.0 %copy-start.44 = (f32[2,16,8,128]{3,2,1,0:T(8,128)S(1)}, f32[2,16,8,128]{3,2,1,0:T(8,128)}, u32[]{:S(2)}) copy-start(f32[2,16,8,128]{3,2,1,0:T(8,128)} %copy-done.43) | copy-start | bytes 393220
  (53 other events, 424.5 us)
where the time goes:
time: 614 us; the launch traced here: 612 us
  blocking collectives  470 us (77%)
  starting transfers between devices  68.9 us (11%)
  other arithmetic  35.3 us (6%)
  waiting for transfers between devices  16.3 us (3%)
  between operations  11.3 us (2%)
  local copies, waits for them, and re-layouts  9.93 us (2%)
    psum x3, blocking collectives, shards(): height = lax.psum(jnp.sum(image * prior), ('gx', 'gy'))  239 us
    psum x3, blocking collectives, global_length(): return jnp.sqrt(lax.psum(jnp.sum(vector * vector), ('gx', 'gy')) + epsilon)  230 us
    ppermute x10, starting transfers between devices, padded_2(): lax.ppermute(lax.slice_in_dim(block, block.shape[dim] - width, None, axis...  50.3 us
    ppermute x10, starting transfers between devices, padded_2(): lax.ppermute(lax.slice_in_dim(block, 0, width, axis=dim), axis, backward)  18.6 us
  transfers between devices with their start and end apart: 20, of which 10 were waited for; matrix products, arithmetic and copies ran while one was open for 1% of the time, Pallas kernels for 0%

commit v1 on v0

v1 whole, which is shorter than its diff:
```python
import functools
import math

import jax
import jax.numpy as jnp
from jax import lax
from jax.experimental import pallas as pl
from jax.experimental.pallas import tpu as pltpu
from jax.sharding import PartitionSpec as P

MESH = pl.DeviceIdType.MESH
CX = 16
EX = 26
OWN = 5
SWEEPS = 6
epsilon = 1e-06


SIDES = [(dx, dy) for dy in (1, -1, 0) for dx in (0, 1, -1) if (dx, dy) != (0, 0)]


def planes(low, high, chunk, body):
    count = (high - low) // chunk

    def group(index, carry):
        body(low + index * chunk)
        return carry

    lax.fori_loop(0, count, group, 0)


def ring_sum(left, a, b, right, rows, lanes):
    a_up, b_up = pltpu.roll(a, 7, 0), pltpu.roll(b, 7, 0)
    a_down, b_down = pltpu.roll(a, 1, 0), pltpu.roll(b, 1, 0)
    y_a = jnp.where(rows == 7, b_up, a_up) + jnp.where(rows == 0, b_down, a_down)
    b_high = jnp.where(rows == 7, a_up, jnp.where(rows == 3, 0.0, b_up))
    b_low = jnp.where(rows == 0, a_down, jnp.where(rows == 4, 0.0, b_down))
    y_b = b_high + b_low
    out_a = (left[0] + right[0]) + (y_a + z_sum(a, lanes))
    out_b = (left[1] + right[1]) + (y_b + z_sum(b, lanes))
    return out_a, out_b


def z_sum(tile, lanes):
    below = jnp.where(lanes == 0, 0.0, pltpu.roll(tile, 1, 1))
    above = jnp.where(lanes == 127, 0.0, pltpu.roll(tile, 127, 1))
    return below + above


def total_rows(tile):
    tile = tile + pltpu.roll(tile, 4, 0)
    tile = tile + pltpu.roll(tile, 2, 0)
    return tile + pltpu.roll(tile, 1, 0)


def total_lanes(tile):
    for shift in (64, 32, 16, 8, 4, 2, 1):
        tile = tile + pltpu.roll(tile, shift, 1)
    return tile


def small_problem(gram):
    ss, s1, s2, d11, d12, d22 = [gram[i : i + 1] for i in range(6)]
    square = ss + epsilon
    beta = jnp.sqrt(square)
    g1 = (epsilon - s1) / square
    h11 = 1.0 - g1
    norm1 = (d11 + 2.0 * g1 * s1 + g1 * g1 * ss) / square
    h21 = jnp.sqrt(jnp.maximum(norm1, 0.0) + epsilon)
    al = 1.0 / (beta * h21)
    ga = g1 * al
    h12 = (al * (s1 + s2) + ga * (ss + s1)) / beta
    v22 = al * al * d11 + 2.0 * al * ga * s1 + ga * ga * ss
    e22 = al * (al * d12 + ga * d11) + ga * (al * s2 + ga * s1)
    h22 = v22 + e22
    x3 = al
    x2 = ga + (1.0 - h22) * al
    x1 = (1.0 - h22) * ga - h12 / beta
    norm2 = (
        x3 * x3 * d22
        + x2 * x2 * d11
        + x1 * x1 * ss
        + 2.0 * (x3 * x2 * d12 + x3 * x1 * s2 + x2 * x1 * s1)
    )
    h32 = jnp.sqrt(jnp.maximum(norm2, 0.0) + epsilon)
    r1 = jnp.sqrt(h11 * h11 + h21 * h21)
    c1, n1 = h11 / r1, h21 / r1
    t0, t1 = c1 * beta, -n1 * beta
    u12 = c1 * h12 + n1 * h22
    low = c1 * h22 - n1 * h12
    r2 = jnp.sqrt(low * low + h32 * h32)
    c2 = low / r2
    y2 = c2 * t1 / r2
    y1 = (t0 - u12 * y2) / r1
    f1 = beta - h11 * y1 - h12 * y2
    f2 = -h21 * y1 - h22 * y2
    f3 = -h32 * y2
    a1, a2 = y1 / beta + y2 * ga, y2 * al
    scale = 1.0 / h32
    v31, v32, v33 = x1 * scale, x2 * scale, x3 * scale
    q1 = f1 / beta + f2 * ga + f3 * v31
    q2 = f2 * al + f3 * v32
    q3 = f3 * v33
    return a1, a2, q1, q2, q3, v31, v32, v33


def kernel(
    scale,
    source_hbm, storage_hbm, ids_hbm, bc_ref, props_ref,
    adjoint_ref, residual_ref, next_ref,
    source, sa, sb, ia, inn, ip, ba, bb,
    ga, gb, gn, gp, ea, eb, m, k_own, lap, recip, rhs, z, fold, keep_p, keep_d,
    rya, ryb, rx, rca, rcb, g1, g2,
    local_sem, s1, r1, s2, r2, s3, r3, s4, r4,
):
    gx, gy = lax.axis_index("gx"), lax.axis_index("gy")
    n_gx, n_gy = lax.axis_size("gx"), lax.axis_size("gy")
    rows = lax.broadcasted_iota(jnp.int32, (8, 128), 0)
    lanes = lax.broadcasted_iota(jnp.int32, (8, 128), 1)
    zero = jnp.zeros((8, 128), jnp.float32)

    def device(dx, dy):
        x = lax.rem(gx + (dx + n_gx), n_gx) if dx else gx
        y = lax.rem(gy + (dy + n_gy), n_gy) if dy else gy
        return x, y

    loads = [
        pltpu.make_async_copy(storage_hbm, sa.at[:, OWN : OWN + CX], local_sem.at[0]),
        pltpu.make_async_copy(ids_hbm, ia.at[OWN : OWN + CX], local_sem.at[1]),
        pltpu.make_async_copy(source_hbm, source, local_sem.at[2]),
    ]
    for copy in loads:
        copy.start()

    size1, size2 = n_gx * 2, n_gy // 2
    me1 = gx * 2 + lax.rem(gy, 2)
    me2 = lax.div(gy, 2)

    def partner1(step):
        other = lax.rem(me1 + step, size1)
        return lax.div(other, 2), lax.div(gy, 2) * 2 + lax.rem(other, 2)

    def partner2(step):
        other = lax.rem(me2 + step, size2)
        return gx, other * 2 + lax.rem(gy, 2)

    barrier = pltpu.get_barrier_semaphore()
    for dx, dy in SIDES:
        pl.semaphore_signal(barrier, inc=1, device_id=device(dx, dy), device_id_type=MESH)

    def greet(step, carry):
        pl.semaphore_signal(barrier, inc=1, device_id=partner1(step), device_id_type=MESH)
        return carry

    def greet2(step, carry):
        pl.semaphore_signal(barrier, inc=1, device_id=partner2(step), device_id_type=MESH)
        return carry

    lax.fori_loop(1, size1, greet, 0)
    lax.fori_loop(1, size2, greet2, 0)

    own_bc = jnp.concatenate(
        [bc_ref[...].astype(jnp.float32), jnp.zeros((8, 112), jnp.float32)], axis=1
    )
    ba[1] = own_bc
    for slot in range(2):
        for field in range(2):
            for tile in range(2):
                z[slot, field, tile, 0] = zero
                z[slot, field, tile, EX - 1] = zero
    for field in range(2):
        for p in list(range(0, OWN)) + list(range(OWN + CX, EX)):
            rhs[field, p] = zero

    pl.semaphore_wait(barrier, len(SIDES) + size1 - 1 + size2 - 1)
    loads[1].wait()
    loads[0].wait()

    first = []
    for dx, dy in SIDES:
        if dx == 0:
            ids_x, ids_to = slice(5, 21), slice(5, 21)
            sto_x, sto_to = ids_x, ids_to
        elif dx == 1:
            ids_x, ids_to = slice(16, 21), slice(0, 5)
            sto_x, sto_to = slice(17, 21), slice(1, 5)
        else:
            ids_x, ids_to = slice(5, 10), slice(21, 26)
            sto_x, sto_to = slice(5, 9), slice(21, 25)
        if dy == 0:
            ids_y, sto_y, ids_dst, sto_dst, bc_dst = slice(0, 8), slice(0, 8), ia, sa, ba
        elif dy == 1:
            ids_y, sto_y, ids_dst, sto_dst, bc_dst = slice(3, 8), slice(4, 8), ip, sb, bb
        else:
            ids_y, sto_y, ids_dst, sto_dst, bc_dst = slice(0, 5), slice(0, 4), inn, sb, bb
        place = 1 - dx
        place = {1: 1, 0: 0, 2: 2}[place]
        moves = [
            (sa.at[:, sto_x, sto_y, :], sto_dst.at[:, sto_to, sto_y, :]),
            (ia.at[ids_x, ids_y, :], ids_dst.at[ids_to, ids_y, :]),
            (ba.at[1, sto_y, :], bc_dst.at[place, sto_y, :]),
        ]
        for src, dst in moves:
            n = len(first)
            copy = pltpu.make_async_remote_copy(
                src_ref=src,
                dst_ref=dst,
                send_sem=s1.at[n],
                recv_sem=r1.at[n],
                device_id=device(dx, dy),
                device_id_type=MESH,
            )
            copy.start()
            first.append(copy)

    def table(row):
        line = jnp.broadcast_to(props_ref[row : row + 1, :], (8, 16))
        return jnp.concatenate([line, jnp.zeros((8, 112), jnp.float32)], axis=1)

    tab_p, tab_t, tab_e = jnp.sqrt(table(0)), jnp.sqrt(table(1)), table(2)

    def look(tab, ids):
        return jnp.take_along_axis(tab, ids, axis=1, mode="promise_in_bounds")

    has_n = (gy < n_gy - 1).astype(jnp.float32)
    has_p = (gy > 0).astype(jnp.float32)

    has_w = (gx > 0).astype(jnp.float32)
    has_e = (gx < n_gx - 1).astype(jnp.float32)
    inside_b = jnp.where(rows < 4, has_n, has_p)

    for copy in first:
        copy.wait_recv()

    def gather(p):
        inside = ((p >= OWN) | (gx > 0)) & ((p < OWN + CX) | (gx < n_gx - 1))
        inside = inside.astype(jnp.float32)
        id_a, id_n, id_p = ia[p], inn[p], ip[p]
        for f, tab in enumerate((tab_p, tab_t)):
            ga[f, p] = look(tab, id_a) * inside
            n_tile = look(tab, id_n) * (inside * has_n)
            p_tile = look(tab, id_p) * (inside * has_p)
            gn[f, p] = n_tile
            gp[f, p] = p_tile
            gb[f, p] = jnp.where(rows < 4, n_tile, p_tile)
        ea[p] = look(tab_e, id_a)
        eb[p] = jnp.where(rows < 4, look(tab_e, id_n), look(tab_e, id_p))

    def gather_two(p):
        gather(p)
        gather(p + 1)

    planes(0, EX, 2, gather_two)

    loads[2].wait()

    def inverse(g_p, g_t, e, lap_p, lap_t, sto):
        sp, spt, stp, st = sto
        first_ = sp + lap_p
        last = st + lap_t
        cross = stp + e * lap_p
        det = 1.0 / (first_ * last - cross * spt)
        k11 = g_p * (last - e * spt) * det
        k12 = g_p * (e * sp - stp) * det
        k21 = -(g_t * spt) * det
        k22 = g_t * first_ * det
        return k11, k12, k21, k22

    def coefficients(p, own):
        west = (p < OWN).astype(jnp.int32)
        east = (p >= OWN + CX).astype(jnp.int32)
        place = 1 - west + east
        lane = p - OWN + 16 * west - 16 * east
        shift = 127 - lane
        top = lanes == 127
        bc_a = jnp.where(top, pltpu.roll(ba[place], shift, 1), 0.0)
        bc_b = jnp.where(top, pltpu.roll(bb[place], shift, 1), 0.0)
        laps_a, laps_b = [], []
        for f in range(2):
            a, b, n_tile, p_tile = ga[f, p], gb[f, p], gn[f, p], gp[f, p]
            a_up, a_down = pltpu.roll(a, 7, 0), pltpu.roll(a, 1, 0)
            b_up, b_down = pltpu.roll(b, 7, 0), pltpu.roll(b, 1, 0)
            y_a = jnp.where(rows == 7, b_up, a_up) + jnp.where(rows == 0, b_down, a_down)
            n_up, n_down = pltpu.roll(n_tile, 7, 0), pltpu.roll(n_tile, 1, 0)
            p_up, p_down = pltpu.roll(p_tile, 7, 0), pltpu.roll(p_tile, 1, 0)
            up = jnp.where(rows < 4, n_up, jnp.where(rows == 7, a_up, p_up))
            down = jnp.where(rows < 4, jnp.where(rows == 0, a_down, n_down), p_down)
            y_b = up + down
            laps_a.append(a * (ga[f, p - 1] + ga[f, p + 1] + y_a + z_sum(a, lanes)))
            laps_b.append(b * (gb[f, p - 1] + gb[f, p + 1] + y_b + z_sum(b, lanes)))
        for tile, (laps, bc, g_ref, e_ref, s_ref) in enumerate(
            ((laps_a, bc_a, ga, ea, sa), (laps_b, bc_b, gb, eb, sb))
        ):
            g_p, g_t, e = g_ref[0, p], g_ref[1, p], e_ref[p]
            lap_p = laps[0] + 2.0 * (g_p * g_p) * bc
            lap_t = laps[1]
            sto = [s_ref[i, p] for i in range(4)]
            k11, k12, k21, k22 = inverse(g_p, g_t, e, lap_p, lap_t, sto)
            m[0, tile, p] = k11 * g_p
            m[1, tile, p] = k12 * g_t
            m[2, tile, p] = k21 * g_p
            m[3, tile, p] = k22 * g_t
            if own and tile == 0:
                x = p - OWN
                for i, value in enumerate((k11, k12, k21, k22)):
                    k_own[i, x] = value
                lap[0, x] = lap_p
                lap[1, x] = sto[3] + lap_t
                recip[0, x] = 1.0 / g_p
                recip[1, x] = 1.0 / g_t
                u, t = source[0, x], source[1, x]
                rhs[0, p] = k11 * u + k12 * t
                rhs[1, p] = k21 * u + k22 * t

    planes(1, OWN, 2, lambda p: [coefficients(p + i, False) for i in range(2)])
    planes(OWN, OWN + CX, 2, lambda p: [coefficients(p + i, True) for i in range(2)])
    planes(OWN + CX, EX - 1, 2, lambda p: [coefficients(p + i, False) for i in range(2)])

    def solve():
        def start(p):
            for i in range(6):
                for f in range(2):
                    z[0, f, 0, p + i] = rhs[f, p + i]
                    z[0, f, 1, p + i] = zero

        planes(1, EX - 1, 6, start)

        def sweep(index, carry):
            old = lax.rem(index, 2)
            new = 1 - old

            def update(p):
                count = 6
                win = [
                    [[z[old, f, tile, p + i - 1] for tile in range(2)] for i in range(count + 2)]
                    for f in range(2)
                ]
                for i in range(count):
                    sums = []
                    for f in range(2):
                        left, mid, right = win[f][i], win[f][i + 1], win[f][i + 2]
                        sums.append(ring_sum(left, mid[0], mid[1], right, rows, lanes))
                    for tile in range(2):
                        sum_q, sum_t = sums[0][tile], sums[1][tile]
                        for f in range(2):
                            value = (
                                m[2 * f, tile, p + i] * sum_q + m[2 * f + 1, tile, p + i] * sum_t
                            )
                            if tile == 0:
                                value = value + rhs[f, p + i]
                            z[new, f, tile, p + i] = value

            planes(1, EX - 1, 6, update)
            return carry

        lax.fori_loop(0, SWEEPS - 1, sweep, 0)

    last_slot = (SWEEPS - 1) % 2

    def exchange(turn, ssem, rsem):
        copies = []
        for dx, dy in SIDES:
            side = 0 if dx == 1 else 1
            wide = slice(20, 25) if dx == 1 else slice(1, 6)
            narrow = slice(21, 25) if dx == 1 else slice(1, 5)
            half = slice(0, 4) if dy == 1 else slice(4, 8)
            line = slice(7, 8) if dy == 1 else slice(0, 1)
            if dy == 0:
                moves = [(z.at[last_slot, :, :, wide], rx.at[turn, side])]
            elif dx == 0:
                moves = [
                    (z.at[last_slot, :, 1, 4:22, half, :], rya.at[turn, :, :, half, :]),
                    (z.at[last_slot, :, 0, 5:21, line, :], ryb.at[turn, :, :, line, :]),
                ]
            else:
                moves = [
                    (z.at[last_slot, :, 1, wide, half, :], rca.at[turn, side, :, :, half, :]),
                    (z.at[last_slot, :, 0, narrow, line, :], rcb.at[turn, side, :, :, line, :]),
                ]
            for src, dst in moves:
                n = len(copies)
                copy = pltpu.make_async_remote_copy(
                    src_ref=src,
                    dst_ref=dst,
                    send_sem=ssem.at[turn, n],
                    recv_sem=rsem.at[turn, n],
                    device_id=device(dx, dy),
                    device_id_type=MESH,
                )
                copy.start()
                copies.append(copy)
        return copies

    def add_up(turn):
        def one(p, west, east):
            for f in range(2):
                a = z[last_slot, f, 0, p] + rya[turn, f, p - 4]
                b = z[last_slot, f, 1, p]
                if west:
                    a = a + (rx[turn, 0, f, 0, p - 4] + rca[turn, 0, f, p - 4])
                if east:
                    a = a + (rx[turn, 1, f, 0, p - 17] + rca[turn, 1, f, p - 17])
                if isinstance(p, int) and p == 4:
                    a = a * has_w
                if isinstance(p, int) and p == 21:
                    a = a * has_e
                fold[f, 0, p - 4] = a
                if not isinstance(p, int) or 5 <= p <= 20:
                    b = b + ryb[turn, f, p - 5]
                    if west:
                        b = b + (rx[turn, 0, f, 1, p - 4] + rcb[turn, 0, f, p - 5])
                    if east:
                        b = b + (rx[turn, 1, f, 1, p - 17] + rcb[turn, 1, f, p - 17])
                    fold[f, 1, p - 4] = b * inside_b

        for p in range(4, 9):
            one(p, True, False)
        planes(9, 17, 4, lambda p: [one(p + i, False, False) for i in range(4)])
        for p in range(17, 22):
            one(p, False, True)

    def apply(turn):
        def one(x, acc):
            i = x + 1
            sums, values = [], []
            for f in range(2):
                a, b = fold[f, 0, i], fold[f, 1, i]
                y_up = jnp.where(rows == 7, pltpu.roll(b, 7, 0), pltpu.roll(a, 7, 0))
                y_down = jnp.where(rows == 0, pltpu.roll(b, 1, 0), pltpu.roll(a, 1, 0))
                near = fold[f, 0, i - 1] + fold[f, 0, i + 1]
                sums.append(near + ((y_up + y_down) + z_sum(a, lanes)))
                values.append(a)
            p = x + OWN
            sp, spt, stp, st = [sa[j, p] for j in range(4)]
            q = values[0] * recip[0, x]
            t = values[1] * recip[1, x]
            u = q - ea[p] * t
            keep_p[turn, 0, x] = u
            keep_p[turn, 1, x] = t
            w_p = sp * u + lap[0, x] * q + stp * t - ga[0, p] * sums[0]
            w_t = spt * u + lap[1, x] * t - ga[1, p] * sums[1]
            src_p, src_t = source[0, x], source[1, x]
            if turn == 0:
                d_p, d_t = w_p - src_p, w_t - src_t
                rhs[0, p] = k_own[0, x] * d_p + k_own[1, x] * d_t
                rhs[1, p] = k_own[2, x] * d_p + k_own[3, x] * d_t
                terms = [(src_p, src_t, src_p, src_t), (src_p, src_t, d_p, d_t), (d_p, d_t, d_p, d_t)]
            else:
                o_p, o_t = keep_d[0, 0, x], keep_d[0, 1, x]
                d_p, d_t = w_p - o_p, w_t - o_t
                terms = [(src_p, src_t, d_p, d_t), (o_p, o_t, d_p, d_t), (d_p, d_t, d_p, d_t)]
            keep_d[turn, 0, x] = d_p
            keep_d[turn, 1, x] = d_t
            return tuple(
                total + (one_ * two + three * four)
                for total, (one_, three, two, four) in zip(acc, terms)
            )

        def group(index, acc):
            for i in range(4):
                acc = one(index * 4 + i, acc)
            return acc

        return lax.fori_loop(0, CX // 4, group, (zero, zero, zero))

    solve()
    copies = exchange(0, s2, r2)
    for copy in copies:
        copy.wait_recv()
    add_up(0)
    dots_a = apply(0)
    for copy in copies:
        copy.wait_send()
    solve()
    copies = exchange(1, s2, r2)
    for copy in copies:
        copy.wait_recv()
    add_up(1)
    dots_b = apply(1)

    ordered = [dots_a[0], dots_a[1], dots_b[0], dots_a[2], dots_b[1], dots_b[2]]
    tile = zero
    for i, part in enumerate(ordered):
        tile = jnp.where(rows == i, total_rows(part), tile)

    def all_sum(tile, box, me, size, partner, ssem, rsem):
        box[me] = tile

        def copy_of(step):
            return pltpu.make_async_remote_copy(
                src_ref=box.at[me],
                dst_ref=box.at[me],
                send_sem=ssem.at[step],
                recv_sem=rsem.at[step],
                device_id=partner(step),
                device_id_type=MESH,
            )

        def send(step, carry):
            copy_of(step).start()
            return carry

        def receive(step, carry):
            copy_of(step).wait_recv()
            return carry

        lax.fori_loop(1, size, send, 0)
        lax.fori_loop(1, size, receive, 0)
        parts = [box[i] for i in range(size)]
        while len(parts) > 1:
            parts = [parts[i] + parts[i + 1] for i in range(0, len(parts), 2)]
        return parts[0], copy_of

    tile, copy1 = all_sum(tile, g1, me1, size1, partner1, s3, r3)
    tile, copy2 = all_sum(tile, g2, me2, size2, partner2, s4, r4)
    factors = small_problem(total_lanes(tile))
    a1, a2, q1, q2, q3, v1, v2, v3 = [jnp.broadcast_to(f, (8, 128)) for f in factors]
    v1, v2, v3 = v1 * scale, v2 * scale, v3 * scale

    def combine(x):
        for i in range(2):
            for f in range(2):
                s, d1, d2 = source[f, x + i], keep_d[0, f, x + i], keep_d[1, f, x + i]
                adjoint_ref[f, x + i] = a1 * keep_p[0, f, x + i] + a2 * keep_p[1, f, x + i]
                residual_ref[f, x + i] = q1 * s + q2 * d1 + q3 * d2
                next_ref[f, x + i] = v1 * s + v2 * d1 + v3 * d2

    planes(0, CX, 2, combine)

    def drain1(step, carry):
        copy1(step).wait_send()
        return carry

    def drain2(step, carry):
        copy2(step).wait_send()
        return carry

    for copy in first:
        copy.wait_send()
    for copy in copies:
        copy.wait_send()
    lax.fori_loop(1, size1, drain1, 0)
    lax.fori_loop(1, size2, drain2, 0)


def shards(adjoint_source, storage, soil_ids, bc_mask, soil_props):
    f32 = jnp.float32
    cells = 2.0 * 16 * lax.axis_size("gx") * 8 * lax.axis_size("gy") * 128
    out = jax.ShapeDtypeStruct(adjoint_source.shape, f32)
    any_spec = pl.BlockSpec(memory_space=pl.ANY)
    vmem = pl.BlockSpec(memory_space=pltpu.VMEM)

    def buf(*lead, dtype=f32):
        return pltpu.VMEM(tuple(lead) + (8, 128), dtype)

    i32 = jnp.int32
    dma = pltpu.SemaphoreType.DMA
    return pl.pallas_call(
        functools.partial(kernel, math.sqrt(cells)),
        out_shape=(out, out, out),
        in_specs=[any_spec, any_spec, any_spec, vmem, vmem],
        out_specs=(vmem, vmem, vmem),
        scratch_shapes=[
            buf(2, CX),
            buf(4, EX), buf(4, EX),
            buf(EX, dtype=i32), buf(EX, dtype=i32), buf(EX, dtype=i32),
            buf(3), buf(3),
            buf(2, EX), buf(2, EX), buf(2, EX), buf(2, EX),
            buf(EX), buf(EX),
            buf(4, 2, EX),
            buf(4, CX), buf(2, CX), buf(2, CX),
            buf(2, EX),
            buf(2, 2, 2, EX),
            buf(2, 2, 18),
            buf(2, 2, CX), buf(2, 2, CX),
            buf(2, 2, 18), buf(2, 2, 16),
            buf(2, 2, 2, 2, 5),
            buf(2, 2, 2, 5), buf(2, 2, 2, 4),
            buf(16), buf(16),
            dma((3,)),
            dma((24,)), dma((24,)),
            dma((2, 14)), dma((2, 14)),
            dma((16,)), dma((16,)),
            dma((16,)), dma((16,)),
        ],
        compiler_params=pltpu.CompilerParams(
            collective_id=0, has_side_effects=True, vmem_limit_bytes=24 << 20
        ),
    )(adjoint_source, storage, soil_ids, bc_mask.T, soil_props)


def solution(mesh):
    in_specs = (
        P(None, "gx", "gy", None),
        P(None, "gx", "gy", None),
        P("gx", "gy", None),
        P("gx", "gy"),
        P(),
    )
    out_specs = (P(None, "gx", "gy", None), P(None, "gx", "gy", None), P(None, "gx", "gy", None))
    return jax.shard_map(shards, mesh=mesh, in_specs=in_specs, out_specs=out_specs, check_vma=False)
```

time: 614 us -> 61.9 us (0.10)
  blocking collectives: 470 us -> 0 us
  starting transfers between devices: 68.9 us -> 0 us
  Pallas kernels: 0 us -> 55 us
  other arithmetic: 35.3 us -> 0 us
  waiting for transfers between devices: 16.3 us -> 0 us
  between operations: 11.3 us -> 0.65 us
    psum x6 -> x0, blocking collectives: 470 us -> none  [the longest x3 239 us: shards(): height = lax.psum(jnp.sum(image * prior), ('gx', 'gy'))]
    ppermute x20 -> x0, starting transfers between devices: 68.9 us -> none  [the longest x10 50.3 us: padded_2(): lax.ppermute(lax.slice_in_dim(block, block.shape[dim] - width, None, axis...]
    pallas_call x0 -> x1, Pallas kernels: none -> 55 us  [shards(): pl.pallas_call(functools.partial(kernel, math.sqrt(cells)), out_shape=(ou...]
    ppermute x20 -> x0, waiting for transfers between devices: 16.3 us -> none  [the longest x10 11 us: padded_2(): lax.ppermute(lax.slice_in_dim(block, block.shape[dim] - width, None, axis...]
    another operation x28 -> x0, other arithmetic: 9.34 us -> none  [the longest x26 9.29 us: apply_adjoint(): return jnp.stack([press_out, heat_out])]
    reduce_sum x6 -> x0, other arithmetic: 9.15 us -> none  [the longest x3 5.82 us: global_length(): return jnp.sqrt(lax.psum(jnp.sum(vector * vector), ('gx', 'gy')) + epsilon)]
    add x41 -> x0, other arithmetic: 6.58 us -> none  [the longest x12 2.58 us: subdomain_solve(): step_p = inverse[0] * remain[0] + inverse[1] * remain[1]]
  transfers between devices with their start and end apart: 20 -> 0, of which waited for: 10 -> 0; matrix products, arithmetic and copies ran while one was open for 1% -> 0% of each run, Pallas kernels for 0% -> 0%
where the time goes in v1:
time: 61.9 us; the launch traced here: 61.7 us
  Pallas kernels  55 us (89%)
  local copies, waits for them, and re-layouts  6.02 us (10%)
  between operations  0.65 us (1%)
    pallas_call x1, Pallas kernels, shards(): pl.pallas_call(functools.partial(kernel, math.sqrt(cells)), out_shape=(ou...  55 us
    unnamed x13, local copies, waits for them, and re-layouts  6.02 us

profile of v1, /device:TPU:1, one launch (start us, length us, event | category | flops | bytes accessed | tf_op | source)
XLA Modules:
  0.0 61.7 jit_solution(10170095282293095720)
XLA Ops:
  0.6 0.0 copy-start
  0.6 0.9 %copy-done = f32[4,16,8,128]{3,2,1,0:T(8,128)S(1)} copy-done((f32[4,16,8,128]{3,2,1,0:T(8,128)S(1)}, f32[4,16,8,128]{3,2,1,0:T(8,128)}, u32[]{:S(2)}) %copy-start) | copy-done | bytes 262168
  1.6 0.0 copy-start.1
  1.6 0.9 %copy-done.1 = f32[2,16,8,128]{3,2,1,0:T(8,128)S(1)} copy-done((f32[2,16,8,128]{3,2,1,0:T(8,128)S(1)}, f32[2,16,8,128]{3,2,1,0:T(8,128)}, u32[]{:S(2)}) %copy-start.1) | copy-done | bytes 131096
  2.5 0.0 copy-start.2
  2.5 0.8 %copy-done.2 = s32[16,8,128]{2,1,0:T(8,128)S(1)} copy-done((s32[16,8,128]{2,1,0:T(8,128)S(1)}, s32[16,8,128]{2,1,0:T(8,128)}, u32[]{:S(2)}) %copy-start.2) | copy-done | bytes 65560
  3.3 0.0 copy-start.3
  3.3 0.7 %copy-done.3 = s32[16,8]{0,1:T(8,128)S(1)} copy-done((s32[16,8]{0,1:T(8,128)S(1)}, s32[16,8]{0,1:T(8,128)}, u32[]{:S(2)}) %copy-start.3) | copy-done | bytes 536
  4.0 0.0 copy-start.4
  4.0 0.7 %copy-done.4 = f32[3,16]{1,0:T(4,128)S(1)} copy-done((f32[3,16]{1,0:T(4,128)S(1)}, f32[3,16]{1,0:T(4,128)}, u32[]{:S(2)}) %copy-start.4) | copy-done | bytes 216
  4.7 55.0 %shard_map.76 = (f32[2,16,8,128]{3,2,1,0:T(8,128)S(1)}, f32[2,16,8,128]{3,2,1,0:T(8,128)S(1)}, f32[2,16,8,128]{3,2,1,0:T(8,128)S(1)}) custom-call(f32[2,16,8,128]{3,2,1,0:T(8,128)S(1)} %copy-done.1, f32[4,16,8,128]{3,2,1,0:T(8,128)S(1)} %copy-done, s32[16,8,128]{2,1,0:T(8,128)S(1)} %copy-done.2, s32[8,16]{1,0:T(8,128)S(1)} %bitcast.1, f32[3,16]{1,0:T(4,128)S(1)} %copy-done.4), custom_call_target="tpu_custom_call" | custom-call | tf_op jit(solution)/shard_map/pallas_call | solution.py:558
  59.7 0.7 %copy.11 = f32[2,16,8,128]{3,2,1,0:T(8,128)} copy(f32[2,16,8,128]{3,2,1,0:T(8,128)S(1)} %get-tuple-element.6) | data formatting | bytes 262144
  60.4 0.7 %copy.12 = f32[2,16,8,128]{3,2,1,0:T(8,128)} copy(f32[2,16,8,128]{3,2,1,0:T(8,128)S(1)} %get-tuple-element.7) | data formatting | bytes 262144
  61.1 0.7 %copy.13 = f32[2,16,8,128]{3,2,1,0:T(8,128)} copy(f32[2,16,8,128]{3,2,1,0:T(8,128)S(1)} %get-tuple-element.8) | data formatting | bytes 262144
Async XLA Ops:
  0.6 1.0 %copy-start = (f32[4,16,8,128]{3,2,1,0:T(8,128)S(1)}, f32[4,16,8,128]{3,2,1,0:T(8,128)}, u32[]{:S(2)}) copy-start(f32[4,16,8,128]{3,2,1,0:T(8,128)} %storage_hbm.1) | copy-start | bytes 786436
  1.6 0.9 %copy-start.1 = (f32[2,16,8,128]{3,2,1,0:T(8,128)S(1)}, f32[2,16,8,128]{3,2,1,0:T(8,128)}, u32[]{:S(2)}) copy-start(f32[2,16,8,128]{3,2,1,0:T(8,128)} %source_hbm.1) | copy-start | bytes 393220
  2.5 0.8 %copy-start.2 = (s32[16,8,128]{2,1,0:T(8,128)S(1)}, s32[16,8,128]{2,1,0:T(8,128)}, u32[]{:S(2)}) copy-start(s32[16,8,128]{2,1,0:T(8,128)} %ids_hbm.1) | copy-start | bytes 196612
  3.3 0.7 %copy-start.3 = (s32[16,8]{0,1:T(8,128)S(1)}, s32[16,8]{0,1:T(8,128)}, u32[]{:S(2)}) copy-start(s32[16,8]{0,1:T(8,128)} %param.8) | copy-start | bytes 1540
  4.0 0.7 %copy-start.4 = (f32[3,16]{1,0:T(4,128)S(1)}, f32[3,16]{1,0:T(4,128)}, u32[]{:S(2)}) copy-start(f32[3,16]{1,0:T(4,128)} %props_ref.1) | copy-start | bytes 580

commit v2 on v1

--- a/solution.py
+++ b/solution.py
@@ -59,7 +59,7 @@
     return tile
 
 
-def small_problem(gram):
+def small_problem(gram, size):
     ss, s1, s2, d11, d12, d22 = [gram[i : i + 1] for i in range(6)]
     square = ss + epsilon
     beta = jnp.sqrt(square)
@@ -96,19 +96,19 @@
     f2 = -h21 * y1 - h22 * y2
     f3 = -h32 * y2
     a1, a2 = y1 / beta + y2 * ga, y2 * al
-    scale = 1.0 / h32
-    v31, v32, v33 = x1 * scale, x2 * scale, x3 * scale
+    inv = 1.0 / h32
+    v31, v32, v33 = x1 * inv, x2 * inv, x3 * inv
     q1 = f1 / beta + f2 * ga + f3 * v31
     q2 = f2 * al + f3 * v32
     q3 = f3 * v33
-    return a1, a2, q1, q2, q3, v31, v32, v33
+    return a1, a2, q1, q2, q3, v31 * size, v32 * size, v33 * size
 
 
 def kernel(
     scale,
-    source_hbm, storage_hbm, ids_hbm, bc_ref, props_ref,
-    adjoint_ref, residual_ref, next_ref,
-    source, sa, sb, ia, inn, ip, ba, bb,
+    source_hbm, storage_hbm, ids_hbm, bc_hbm, props_hbm,
+    p1_hbm, p2_hbm, d1_hbm, d2_hbm, factors_ref,
+    bc_ref, props_ref, source, sa, sb, ia, inn, ip, ba, bb,
     ga, gb, gn, gp, ea, eb, m, k_own, lap, recip, rhs, z, fold, keep_p, keep_d,
     rya, ryb, rx, rca, rcb, g1, g2,
     local_sem, s1, r1, s2, r2, s3, r3, s4, r4,
@@ -128,21 +128,23 @@
         pltpu.make_async_copy(storage_hbm, sa.at[:, OWN : OWN + CX], local_sem.at[0]),
         pltpu.make_async_copy(ids_hbm, ia.at[OWN : OWN + CX], local_sem.at[1]),
         pltpu.make_async_copy(source_hbm, source, local_sem.at[2]),
+        pltpu.make_async_copy(bc_hbm, bc_ref, local_sem.at[3]),
+        pltpu.make_async_copy(props_hbm, props_ref, local_sem.at[4]),
     ]
     for copy in loads:
         copy.start()
 
-    size1, size2 = n_gx * 2, n_gy // 2
-    me1 = gx * 2 + lax.rem(gy, 2)
-    me2 = lax.div(gy, 2)
+    size1, size2 = n_gx * 4, n_gy // 4
+    me1 = gx * 4 + lax.rem(gy, 4)
+    me2 = lax.div(gy, 4)
 
     def partner1(step):
         other = lax.rem(me1 + step, size1)
-        return lax.div(other, 2), lax.div(gy, 2) * 2 + lax.rem(other, 2)
+        return lax.div(other, 4), me2 * 4 + lax.rem(other, 4)
 
     def partner2(step):
         other = lax.rem(me2 + step, size2)
-        return gx, other * 2 + lax.rem(gy, 2)
+        return gx, other * 4 + lax.rem(gy, 4)
 
     barrier = pltpu.get_barrier_semaphore()
     for dx, dy in SIDES:
@@ -159,6 +161,7 @@
     lax.fori_loop(1, size1, greet, 0)
     lax.fori_loop(1, size2, greet2, 0)
 
+    loads[3].wait()
     own_bc = jnp.concatenate(
         [bc_ref[...].astype(jnp.float32), jnp.zeros((8, 112), jnp.float32)], axis=1
     )
@@ -174,44 +177,39 @@
 
     pl.semaphore_wait(barrier, len(SIDES) + size1 - 1 + size2 - 1)
     loads[1].wait()
+
+    first = []
+
+    def push(src, dst, dx, dy):
+        n = len(first)
+        copy = pltpu.make_async_remote_copy(
+            src_ref=src,
+            dst_ref=dst,
+            send_sem=s1.at[n],
+            recv_sem=r1.at[n],
+            device_id=device(dx, dy),
+            device_id_type=MESH,
+        )
+        copy.start()
+        first.append(copy)
+
+    for dx, dy in SIDES:
+        src_x = {0: slice(5, 21), 1: slice(16, 21), -1: slice(5, 10)}[dx]
+        dst_x = {0: slice(5, 21), 1: slice(0, 5), -1: slice(21, 26)}[dx]
+        y = {0: slice(0, 8), 1: slice(3, 8), -1: slice(0, 5)}[dy]
+        half = {0: slice(0, 8), 1: slice(4, 8), -1: slice(0, 4)}[dy]
+        place = {0: 1, 1: 0, -1: 2}[dx]
+        push(ia.at[src_x, y, :], {0: ia, 1: ip, -1: inn}[dy].at[dst_x, y, :], dx, dy)
+        push(ba.at[1, half, :], (bb if dy else ba).at[place, half, :], dx, dy)
+    n_ids = len(first)
     loads[0].wait()
-
-    first = []
     for dx, dy in SIDES:
-        if dx == 0:
-            ids_x, ids_to = slice(5, 21), slice(5, 21)
-            sto_x, sto_to = ids_x, ids_to
-        elif dx == 1:
-            ids_x, ids_to = slice(16, 21), slice(0, 5)
-            sto_x, sto_to = slice(17, 21), slice(1, 5)
-        else:
-            ids_x, ids_to = slice(5, 10), slice(21, 26)
-            sto_x, sto_to = slice(5, 9), slice(21, 25)
-        if dy == 0:
-            ids_y, sto_y, ids_dst, sto_dst, bc_dst = slice(0, 8), slice(0, 8), ia, sa, ba
-        elif dy == 1:
-            ids_y, sto_y, ids_dst, sto_dst, bc_dst = slice(3, 8), slice(4, 8), ip, sb, bb
-        else:
-            ids_y, sto_y, ids_dst, sto_dst, bc_dst = slice(0, 5), slice(0, 4), inn, sb, bb
-        place = 1 - dx
-        place = {1: 1, 0: 0, 2: 2}[place]
-        moves = [
-            (sa.at[:, sto_x, sto_y, :], sto_dst.at[:, sto_to, sto_y, :]),
-            (ia.at[ids_x, ids_y, :], ids_dst.at[ids_to, ids_y, :]),
-            (ba.at[1, sto_y, :], bc_dst.at[place, sto_y, :]),
-        ]
-        for src, dst in moves:
-            n = len(first)
-            copy = pltpu.make_async_remote_copy(
-                src_ref=src,
-                dst_ref=dst,
-                send_sem=s1.at[n],
-                recv_sem=r1.at[n],
-                device_id=device(dx, dy),
-                device_id_type=MESH,
-            )
-            copy.start()
-            first.append(copy)
+        src_x = {0: slice(5, 21), 1: slice(17, 21), -1: slice(5, 9)}[dx]
+        dst_x = {0: slice(5, 21), 1: slice(1, 5), -1: slice(21, 25)}[dx]
+        half = {0: slice(0, 8), 1: slice(4, 8), -1: slice(0, 4)}[dy]
+        push(sa.at[:, src_x, half, :], (sb if dy else sa).at[:, dst_x, half, :], dx, dy)
+
+    loads[4].wait()
 
     def table(row):
         line = jnp.broadcast_to(props_ref[row : row + 1, :], (8, 16))
@@ -229,7 +227,7 @@
     has_e = (gx < n_gx - 1).astype(jnp.float32)
     inside_b = jnp.where(rows < 4, has_n, has_p)
 
-    for copy in first:
+    for copy in first[:n_ids]:
         copy.wait_recv()
 
     def gather(p):
@@ -266,16 +264,13 @@
         k22 = g_t * first_ * det
         return k11, k12, k21, k22
 
-    def coefficients(p, own):
+    def diagonals(p):
         west = (p < OWN).astype(jnp.int32)
         east = (p >= OWN + CX).astype(jnp.int32)
         place = 1 - west + east
-        lane = p - OWN + 16 * west - 16 * east
-        shift = 127 - lane
+        shift = 127 - (p - OWN + 16 * west - 16 * east)
         top = lanes == 127
-        bc_a = jnp.where(top, pltpu.roll(ba[place], shift, 1), 0.0)
-        bc_b = jnp.where(top, pltpu.roll(bb[place], shift, 1), 0.0)
-        laps_a, laps_b = [], []
+        bounds = [jnp.where(top, pltpu.roll(ref[place], shift, 1), 0.0) for ref in (ba, bb)]
         for f in range(2):
             a, b, n_tile, p_tile = ga[f, p], gb[f, p], gn[f, p], gp[f, p]
             a_up, a_down = pltpu.roll(a, 7, 0), pltpu.roll(a, 1, 0)
@@ -286,35 +281,40 @@
             up = jnp.where(rows < 4, n_up, jnp.where(rows == 7, a_up, p_up))
             down = jnp.where(rows < 4, jnp.where(rows == 0, a_down, n_down), p_down)
             y_b = up + down
-            laps_a.append(a * (ga[f, p - 1] + ga[f, p + 1] + y_a + z_sum(a, lanes)))
-            laps_b.append(b * (gb[f, p - 1] + gb[f, p + 1] + y_b + z_sum(b, lanes)))
-        for tile, (laps, bc, g_ref, e_ref, s_ref) in enumerate(
-            ((laps_a, bc_a, ga, ea, sa), (laps_b, bc_b, gb, eb, sb))
-        ):
-            g_p, g_t, e = g_ref[0, p], g_ref[1, p], e_ref[p]
-            lap_p = laps[0] + 2.0 * (g_p * g_p) * bc
-            lap_t = laps[1]
-            sto = [s_ref[i, p] for i in range(4)]
-            k11, k12, k21, k22 = inverse(g_p, g_t, e, lap_p, lap_t, sto)
-            m[0, tile, p] = k11 * g_p
-            m[1, tile, p] = k12 * g_t
-            m[2, tile, p] = k21 * g_p
-            m[3, tile, p] = k22 * g_t
-            if own and tile == 0:
-                x = p - OWN
-                for i, value in enumerate((k11, k12, k21, k22)):
-                    k_own[i, x] = value
-                lap[0, x] = lap_p
-                lap[1, x] = sto[3] + lap_t
-                recip[0, x] = 1.0 / g_p
-                recip[1, x] = 1.0 / g_t
-                u, t = source[0, x], source[1, x]
-                rhs[0, p] = k11 * u + k12 * t
-                rhs[1, p] = k21 * u + k22 * t
-
-    planes(1, OWN, 2, lambda p: [coefficients(p + i, False) for i in range(2)])
-    planes(OWN, OWN + CX, 2, lambda p: [coefficients(p + i, True) for i in range(2)])
-    planes(OWN + CX, EX - 1, 2, lambda p: [coefficients(p + i, False) for i in range(2)])
+            lap_a = a * (ga[f, p - 1] + ga[f, p + 1] + y_a + z_sum(a, lanes))
+            lap_b = b * (gb[f, p - 1] + gb[f, p + 1] + y_b + z_sum(b, lanes))
+            if f == 0:
+                lap_a = lap_a + 2.0 * (a * a) * bounds[0]
+                lap_b = lap_b + 2.0 * (b * b) * bounds[1]
+            lap[f, 0, p] = lap_a
+            lap[f, 1, p] = lap_b
+
+    def invert(p, tile, own):
+        g_ref, e_ref, s_ref = ((ga, ea, sa), (gb, eb, sb))[tile]
+        g_p, g_t, e = g_ref[0, p], g_ref[1, p], e_ref[p]
+        sto = [s_ref[i, p] for i in range(4)]
+        k11, k12, k21, k22 = inverse(g_p, g_t, e, lap[0, tile, p], lap[1, tile, p], sto)
+        m[0, tile, p] = k11 * g_p
+        m[1, tile, p] = k12 * g_t
+        m[2, tile, p] = k21 * g_p
+        m[3, tile, p] = k22 * g_t
+        if own:
+            x = p - OWN
+            for i, value in enumerate((k11, k12, k21, k22)):
+                k_own[i, x] = value
+            recip[0, x] = 1.0 / g_p
+            recip[1, x] = 1.0 / g_t
+            u, t = source[0, x], source[1, x]
+            rhs[0, p] = k11 * u + k12 * t
+            rhs[1, p] = k21 * u + k22 * t
+
+    planes(1, EX - 1, 2, lambda p: [diagonals(p + i) for i in range(2)])
+    planes(OWN, OWN + CX, 4, lambda p: [invert(p + i, 0, True) for i in range(4)])
+    for copy in first[n_ids:]:
+        copy.wait_recv()
+    planes(1, EX - 1, 4, lambda p: [invert(p + i, 1, False) for i in range(4)])
+    planes(1, OWN, 4, lambda p: [invert(p + i, 0, False) for i in range(4)])
+    planes(OWN + CX, EX - 1, 4, lambda p: [invert(p + i, 0, False) for i in range(4)])
 
     def solve():
         def start(p):
@@ -363,10 +363,18 @@
             side = 0 if dx == 1 else 1
             wide = slice(20, 25) if dx == 1 else slice(1, 6)
             narrow = slice(21, 25) if dx == 1 else slice(1, 5)
+            narrow_to = slice(1, 5) if dx == 1 else slice(0, 4)
             half = slice(0, 4) if dy == 1 else slice(4, 8)
             line = slice(7, 8) if dy == 1 else slice(0, 1)
             if dy == 0:
-                moves = [(z.at[last_slot, :, :, wide], rx.at[turn, side])]
+                moves = [(z.at[last_slot, :, 0, wide], rx.at[turn, side, :, 0])]
+                for edge in (slice(0, 1), slice(7, 8)):
+                    moves.append(
+                        (
+                            z.at[last_slot, :, 1, narrow, edge, :],
+                            rx.at[turn, side, :, 1, narrow_to, edge, :],
+                        )
+                    )
             elif dx == 0:
                 moves = [
                     (z.at[last_slot, :, 1, 4:22, half, :], rya.at[turn, :, :, half, :]),
@@ -437,8 +445,8 @@
             u = q - ea[p] * t
             keep_p[turn, 0, x] = u
             keep_p[turn, 1, x] = t
-            w_p = sp * u + lap[0, x] * q + stp * t - ga[0, p] * sums[0]
-            w_t = spt * u + lap[1, x] * t - ga[1, p] * sums[1]
+            w_p = sp * u + lap[0, 0, p] * q + stp * t - ga[0, p] * sums[0]
+            w_t = spt * u + (st + lap[1, 0, p]) * t - ga[1, p] * sums[1]
             src_p, src_t = source[0, x], source[1, x]
             if turn == 0:
                 d_p, d_t = w_p - src_p, w_t - src_t
@@ -463,12 +471,18 @@
 
         return lax.fori_loop(0, CX // 4, group, (zero, zero, zero))
 
+    def store(src, dst, n):
+        copy = pltpu.make_async_copy(src, dst, local_sem.at[n])
+        copy.start()
+        return copy
+
     solve()
     copies = exchange(0, s2, r2)
     for copy in copies:
         copy.wait_recv()
     add_up(0)
     dots_a = apply(0)
+    stores = [store(keep_p.at[0], p1_hbm, 5), store(keep_d.at[0], d1_hbm, 6)]
     for copy in copies:
         copy.wait_send()
     solve()
@@ -477,11 +491,13 @@
         copy.wait_recv()
     add_up(1)
     dots_b = apply(1)
+    stores += [store(keep_p.at[1], p2_hbm, 7), store(keep_d.at[1], d2_hbm, 8)]
 
     ordered = [dots_a[0], dots_a[1], dots_b[0], dots_a[2], dots_b[1], dots_b[2]]
     tile = zero
     for i, part in enumerate(ordered):
         tile = jnp.where(rows == i, total_rows(part), tile)
+    tile = total_rows(jnp.where(rows == lanes, total_lanes(tile), 0.0))[0:1]
 
     def all_sum(tile, box, me, size, partner, ssem, rsem):
         box[me] = tile
@@ -513,19 +529,11 @@
 
     tile, copy1 = all_sum(tile, g1, me1, size1, partner1, s3, r3)
     tile, copy2 = all_sum(tile, g2, me2, size2, partner2, s4, r4)
-    factors = small_problem(total_lanes(tile))
-    a1, a2, q1, q2, q3, v1, v2, v3 = [jnp.broadcast_to(f, (8, 128)) for f in factors]
-    v1, v2, v3 = v1 * scale, v2 * scale, v3 * scale
-
-    def combine(x):
-        for i in range(2):
-            for f in range(2):
-                s, d1, d2 = source[f, x + i], keep_d[0, f, x + i], keep_d[1, f, x + i]
-                adjoint_ref[f, x + i] = a1 * keep_p[0, f, x + i] + a2 * keep_p[1, f, x + i]
-                residual_ref[f, x + i] = q1 * s + q2 * d1 + q3 * d2
-                next_ref[f, x + i] = v1 * s + v2 * d1 + v3 * d2
-
-    planes(0, CX, 2, combine)
+    factors = small_problem(total_lanes(jnp.where(rows == lanes, tile, 0.0)), scale)
+    table_out = zero
+    for i, factor in enumerate(factors):
+        table_out = jnp.where(rows == i, factor, table_out)
+    factors_ref[...] = table_out
 
     def drain1(step, carry):
         copy1(step).wait_send()
@@ -535,6 +543,8 @@
         copy2(step).wait_send()
         return carry
 
+    for copy in stores:
+        copy.wait()
     for copy in first:
         copy.wait_send()
     for copy in copies:
@@ -547,7 +557,7 @@
     f32 = jnp.float32
     cells = 2.0 * 16 * lax.axis_size("gx") * 8 * lax.axis_size("gy") * 128
     out = jax.ShapeDtypeStruct(adjoint_source.shape, f32)
-    any_spec = pl.BlockSpec(memory_space=pl.ANY)
+    any_spec = pl.BlockSpec(memory_space=pltpu.HBM)
     vmem = pl.BlockSpec(memory_space=pltpu.VMEM)
 
     def buf(*lead, dtype=f32):
@@ -555,12 +565,13 @@
 
     i32 = jnp.int32
     dma = pltpu.SemaphoreType.DMA
-    return pl.pallas_call(
+    p1, p2, d1, d2, factors = pl.pallas_call(
         functools.partial(kernel, math.sqrt(cells)),
-        out_shape=(out, out, out),
-        in_specs=[any_spec, any_spec, any_spec, vmem, vmem],
-        out_specs=(vmem, vmem, vmem),
+        out_shape=(out, out, out, out, jax.ShapeDtypeStruct((8, 128), f32)),
+        in_specs=[any_spec] * 5,
+        out_specs=(any_spec,) * 4 + (vmem,),
         scratch_shapes=[
+            pltpu.VMEM((8, CX), i32), pltpu.VMEM((3, 16), f32),
             buf(2, CX),
             buf(4, EX), buf(4, EX),
             buf(EX, dtype=i32), buf(EX, dtype=i32), buf(EX, dtype=i32),
@@ -568,7 +579,7 @@
             buf(2, EX), buf(2, EX), buf(2, EX), buf(2, EX),
             buf(EX), buf(EX),
             buf(4, 2, EX),
-            buf(4, CX), buf(2, CX), buf(2, CX),
+            buf(4, CX), buf(2, 2, EX), buf(2, CX),
             buf(2, EX),
             buf(2, 2, 2, EX),
             buf(2, 2, 18),
@@ -576,17 +587,22 @@
             buf(2, 2, 18), buf(2, 2, 16),
             buf(2, 2, 2, 2, 5),
             buf(2, 2, 2, 5), buf(2, 2, 2, 4),
-            buf(16), buf(16),
-            dma((3,)),
+            pltpu.VMEM((32, 1, 128), f32), pltpu.VMEM((8, 1, 128), f32),
+            dma((9,)),
             dma((24,)), dma((24,)),
-            dma((2, 14)), dma((2, 14)),
-            dma((16,)), dma((16,)),
-            dma((16,)), dma((16,)),
+            dma((2, 18)), dma((2, 18)),
+            dma((32,)), dma((32,)),
+            dma((8,)), dma((8,)),
         ],
         compiler_params=pltpu.CompilerParams(
-            collective_id=0, has_side_effects=True, vmem_limit_bytes=24 << 20
+            collective_id=0, has_side_effects=True, vmem_limit_bytes=60 << 20
         ),
     )(adjoint_source, storage, soil_ids, bc_mask.T, soil_props)
+    c = [factors[i] for i in range(8)]
+    adjoint = c[0] * p1 + c[1] * p2
+    residual = c[2] * adjoint_source + c[3] * d1 + c[4] * d2
+    next_basis = c[5] * adjoint_source + c[6] * d1 + c[7] * d2
+    return adjoint, residual, next_basis
 
 
 def solution(mesh):

time: 61.9 us -> 55.1 us (0.89)
  local copies, waits for them, and re-layouts: 6.02 us -> 0.68 us
  Pallas kernels: 55 us -> 51.7 us
  other arithmetic: 0 us -> 1.88 us
    unnamed x13 -> x4, local copies, waits for them, and re-layouts: 6.02 us -> 0.67 us
    pallas_call x1, Pallas kernels: 55 us -> 51.7 us  [shards(): pl.pallas_call(functools.partial(kernel, math.sqrt(cells)), out_shape=(ou...]
    add x0 -> x1, other arithmetic: none -> 1.88 us  [shards(): next_basis = c[5] * adjoint_source + c[6] * d1 + c[7] * d2]
where the time goes in v2:
time: 55.1 us; the launch traced here: 54.9 us
  Pallas kernels  51.7 us (94%)
  other arithmetic  1.88 us (3%)
  local copies, waits for them, and re-layouts  0.68 us (1%)
  between operations  0.66 us (1%)
    pallas_call x1, Pallas kernels, shards(): pl.pallas_call(functools.partial(kernel, math.sqrt(cells)), out_shape=(ou...  51.7 us
    add x1, other arithmetic, shards(): next_basis = c[5] * adjoint_source + c[6] * d1 + c[7] * d2  1.88 us

profile of v2, /device:TPU:1, one launch (start us, length us, event | category | flops | bytes accessed | tf_op | source)
XLA Modules:
  0.0 54.9 jit_solution(8011582973283244423)
XLA Ops:
  0.6 0.0 copy-start
  0.6 51.7 %shard_map.76 = (f32[2,16,8,128]{3,2,1,0:T(8,128)}, f32[2,16,8,128]{3,2,1,0:T(8,128)}, f32[2,16,8,128]{3,2,1,0:T(8,128)}, f32[2,16,8,128]{3,2,1,0:T(8,128)}, f32[8,128]{1,0:T(8,128)}) custom-call(f32[2,16,8,128]{3,2,1,0:T(8,128)} %source_hbm.1, f32[4,16,8,128]{3,2,1,0:T(8,128)} %storage_hbm.1, s32[16,8,128]{2,1,0:T(8,128)} %ids_hbm.1, s32[8,16]{1,0:T(8,128)} %bitcast.17, ...), custom_call_target="tpu_custom_call" | custom-call | tf_op jit(solution)/shard_map/pallas_call | solution.py:568
  52.3 0.0 copy-start.1
  52.4 0.7 %copy-done.1 = f32[8,128]{1,0:T(8,128)S(1)} copy-done((f32[8,128]{1,0:T(8,128)S(1)}, f32[8,128]{1,0:T(8,128)}, u32[]{:S(2)}) %copy-start.1) | copy-done | bytes 4120
  53.0 0.0 copy-done
  53.0 1.9 %multiply_add_fusion = (f32[2,16,8,128]{3,2,1,0:T(8,128)}, f32[2,16,8,128]{3,2,1,0:T(8,128)}, f32[2,16,8,128]{3,2,1,0:T(8,128)}) fusion(f32[2,16,8,128]{3,2,1,0:T(8,128)} %get-tuple-element.12, f32[2,16,8,128]{3,2,1,0:T(8,128)} %get-tuple-element.11, f32[2,16,8,128]{3,2,1,0:T(8,128)S(1)} %copy-done, f32[128]{0:T(128)S(1)} %get-tuple-element.16, ...), kind=kLoop, calls=%fused_computation | loop fusion | flops 425984 | bytes 1052672 | tf_op jit(solution)/shard_map/add | solution.py:604
  (1 shorter events, 0.0 us)
Async XLA Ops:
  0.6 52.4 %copy-start = (f32[2,16,8,128]{3,2,1,0:T(8,128)S(1)}, f32[2,16,8,128]{3,2,1,0:T(8,128)}, u32[]{:S(2)}) copy-start(f32[2,16,8,128]{3,2,1,0:T(8,128)} %source_hbm.1) | copy-start | bytes 393220
  52.3 0.7 %copy-start.1 = (f32[8,128]{1,0:T(8,128)S(1)}, f32[8,128]{1,0:T(8,128)}, u32[]{:S(2)}) copy-start(f32[8,128]{1,0:T(8,128)} %get-tuple-element.8) | copy-start | bytes 12292

commit v3 on v2

--- a/solution.py
+++ b/solution.py
@@ -107,9 +107,9 @@
 def kernel(
     scale,
     source_hbm, storage_hbm, ids_hbm, bc_hbm, props_hbm,
-    p1_hbm, p2_hbm, d1_hbm, d2_hbm, factors_ref,
+    p1, p2, d1, d2, factors_ref,
     bc_ref, props_ref, source, sa, sb, ia, inn, ip, ba, bb,
-    ga, gb, gn, gp, ea, eb, m, k_own, lap, recip, rhs, z, fold, keep_p, keep_d,
+    ga, gb, gn, gp, ea, eb, m, k_own, lap, recip, rhs, z, fold,
     rya, ryb, rx, rca, rcb, g1, g2,
     local_sem, s1, r1, s2, r2, s3, r3, s4, r4,
 ):
@@ -118,6 +118,7 @@
     rows = lax.broadcasted_iota(jnp.int32, (8, 128), 0)
     lanes = lax.broadcasted_iota(jnp.int32, (8, 128), 1)
     zero = jnp.zeros((8, 128), jnp.float32)
+    keep_p, keep_d = (p1, p2), (d1, d2)
 
     def device(dx, dy):
         x = lax.rem(gx + (dx + n_gx), n_gx) if dx else gx
@@ -330,15 +331,14 @@
             new = 1 - old
 
             def update(p):
-                count = 6
-                win = [
-                    [[z[old, f, tile, p + i - 1] for tile in range(2)] for i in range(count + 2)]
-                    for f in range(2)
-                ]
+                count = 24
+                def load(f, i):
+                    return [z[old, f, tile, p + i - 1] for tile in range(2)]
+
                 for i in range(count):
                     sums = []
                     for f in range(2):
-                        left, mid, right = win[f][i], win[f][i + 1], win[f][i + 2]
+                        left, mid, right = load(f, i), load(f, i + 1), load(f, i + 2)
                         sums.append(ring_sum(left, mid[0], mid[1], right, rows, lanes))
                     for tile in range(2):
                         sum_q, sum_t = sums[0][tile], sums[1][tile]
@@ -350,7 +350,7 @@
                                 value = value + rhs[f, p + i]
                             z[new, f, tile, p + i] = value
 
-            planes(1, EX - 1, 6, update)
+            update(1)
             return carry
 
         lax.fori_loop(0, SWEEPS - 1, sweep, 0)
@@ -443,8 +443,8 @@
             q = values[0] * recip[0, x]
             t = values[1] * recip[1, x]
             u = q - ea[p] * t
-            keep_p[turn, 0, x] = u
-            keep_p[turn, 1, x] = t
+            keep_p[turn][0, x] = u
+            keep_p[turn][1, x] = t
             w_p = sp * u + lap[0, 0, p] * q + stp * t - ga[0, p] * sums[0]
             w_t = spt * u + (st + lap[1, 0, p]) * t - ga[1, p] * sums[1]
             src_p, src_t = source[0, x], source[1, x]
@@ -454,11 +454,11 @@
                 rhs[1, p] = k_own[2, x] * d_p + k_own[3, x] * d_t
                 terms = [(src_p, src_t, src_p, src_t), (src_p, src_t, d_p, d_t), (d_p, d_t, d_p, d_t)]
             else:
-                o_p, o_t = keep_d[0, 0, x], keep_d[0, 1, x]
+                o_p, o_t = keep_d[0][0, x], keep_d[0][1, x]
                 d_p, d_t = w_p - o_p, w_t - o_t
                 terms = [(src_p, src_t, d_p, d_t), (o_p, o_t, d_p, d_t), (d_p, d_t, d_p, d_t)]
-            keep_d[turn, 0, x] = d_p
-            keep_d[turn, 1, x] = d_t
+            keep_d[turn][0, x] = d_p
+            keep_d[turn][1, x] = d_t
             return tuple(
                 total + (one_ * two + three * four)
                 for total, (one_, three, two, four) in zip(acc, terms)
@@ -470,11 +470,6 @@
             return acc
 
         return lax.fori_loop(0, CX // 4, group, (zero, zero, zero))
-
-    def store(src, dst, n):
-        copy = pltpu.make_async_copy(src, dst, local_sem.at[n])
-        copy.start()
-        return copy
 
     solve()
     copies = exchange(0, s2, r2)
@@ -482,7 +477,6 @@
         copy.wait_recv()
     add_up(0)
     dots_a = apply(0)
-    stores = [store(keep_p.at[0], p1_hbm, 5), store(keep_d.at[0], d1_hbm, 6)]
     for copy in copies:
         copy.wait_send()
     solve()
@@ -491,7 +485,6 @@
         copy.wait_recv()
     add_up(1)
     dots_b = apply(1)
-    stores += [store(keep_p.at[1], p2_hbm, 7), store(keep_d.at[1], d2_hbm, 8)]
 
     ordered = [dots_a[0], dots_a[1], dots_b[0], dots_a[2], dots_b[1], dots_b[2]]
     tile = zero
@@ -543,8 +536,6 @@
         copy2(step).wait_send()
         return carry
 
-    for copy in stores:
-        copy.wait()
     for copy in first:
         copy.wait_send()
     for copy in copies:
@@ -556,7 +547,7 @@
 def shards(adjoint_source, storage, soil_ids, bc_mask, soil_props):
     f32 = jnp.float32
     cells = 2.0 * 16 * lax.axis_size("gx") * 8 * lax.axis_size("gy") * 128
-    out = jax.ShapeDtypeStruct(adjoint_source.shape, f32)
+    out = pltpu.VMEM(adjoint_source.shape, f32)
     any_spec = pl.BlockSpec(memory_space=pltpu.HBM)
     vmem = pl.BlockSpec(memory_space=pltpu.VMEM)
 
@@ -567,9 +558,9 @@
     dma = pltpu.SemaphoreType.DMA
     p1, p2, d1, d2, factors = pl.pallas_call(
         functools.partial(kernel, math.sqrt(cells)),
-        out_shape=(out, out, out, out, jax.ShapeDtypeStruct((8, 128), f32)),
+        out_shape=(out, out, out, out, pltpu.VMEM((8, 128), f32)),
         in_specs=[any_spec] * 5,
-        out_specs=(any_spec,) * 4 + (vmem,),
+        out_specs=(vmem,) * 5,
         scratch_shapes=[
             pltpu.VMEM((8, CX), i32), pltpu.VMEM((3, 16), f32),
             buf(2, CX),
@@ -583,12 +574,11 @@
             buf(2, EX),
             buf(2, 2, 2, EX),
             buf(2, 2, 18),
-            buf(2, 2, CX), buf(2, 2, CX),
             buf(2, 2, 18), buf(2, 2, 16),
             buf(2, 2, 2, 2, 5),
             buf(2, 2, 2, 5), buf(2, 2, 2, 4),
             pltpu.VMEM((32, 1, 128), f32), pltpu.VMEM((8, 1, 128), f32),
-            dma((9,)),
+            dma((5,)),
             dma((24,)), dma((24,)),
             dma((2, 18)), dma((2, 18)),
             dma((32,)), dma((32,)),

time: 55.1 us -> 51.1 us (0.927)
  Pallas kernels: 51.7 us -> 49.6 us
  other arithmetic: 1.88 us -> 0.78 us
  local copies, waits for them, and re-layouts: 0.68 us -> 0.01 us
    pallas_call x1, Pallas kernels: 51.7 us -> 49.6 us  [shards(): pl.pallas_call(functools.partial(kernel, math.sqrt(cells)), out_shape=(ou...]
    add x1, other arithmetic: 1.88 us -> 0.78 us  [shards(): next_basis = c[5] * adjoint_source + c[6] * d1 + c[7] * d2]
    unnamed x4 -> x2, local copies, waits for them, and re-layouts: 0.67 us -> 0.01 us
where the time goes in v3:
time: 51.1 us; the launch traced here: 51 us
  Pallas kernels  49.6 us (97%)
  other arithmetic  0.78 us (2%)
  between operations  0.66 us (1%)
    pallas_call x1, Pallas kernels, shards(): pl.pallas_call(functools.partial(kernel, math.sqrt(cells)), out_shape=(ou...  49.6 us

profile of v3, /device:TPU:1, one launch (start us, length us, event | category | flops | bytes accessed | tf_op | source)
XLA Modules:
  0.0 51.0 jit_solution(18173015610617513808)
XLA Ops:
  0.6 0.0 copy-start
  0.6 49.6 %shard_map.76 = (f32[2,16,8,128]{3,2,1,0:T(8,128)S(1)}, f32[2,16,8,128]{3,2,1,0:T(8,128)S(1)}, f32[2,16,8,128]{3,2,1,0:T(8,128)S(1)}, f32[2,16,8,128]{3,2,1,0:T(8,128)S(1)}, f32[8,128]{1,0:T(8,128)S(1)}) custom-call(f32[2,16,8,128]{3,2,1,0:T(8,128)} %source_hbm.1, f32[4,16,8,128]{3,2,1,0:T(8,128)} %storage_hbm.1, s32[16,8,128]{2,1,0:T(8,128)} %ids_hbm.1, ...), custom_call_target="tpu_custom_call" | custom-call | tf_op jit(solution)/shard_map/pallas_call | solution.py:559
  50.2 0.0 copy-done
  50.2 0.8 %multiply_add_fusion = (f32[2,16,8,128]{3,2,1,0:T(8,128)}, f32[2,16,8,128]{3,2,1,0:T(8,128)}, f32[2,16,8,128]{3,2,1,0:T(8,128)}) fusion(f32[2,16,8,128]{3,2,1,0:T(8,128)S(1)} %get-tuple-element.12, f32[2,16,8,128]{3,2,1,0:T(8,128)S(1)} %get-tuple-element.11, f32[2,16,8,128]{3,2,1,0:T(8,128)S(1)} %copy-done, f32[128]{0:T(128)S(1)} %get-tuple-element.16, ...), kind=kLoop, calls=%fused_computation | loop fusion | flops 425984 | bytes 1052672 | tf_op jit(solution)/shard_map/add | solution.py:594
  (1 shorter events, 0.0 us)
Async XLA Ops:
  0.6 49.6 %copy-start = (f32[2,16,8,128]{3,2,1,0:T(8,128)S(1)}, f32[2,16,8,128]{3,2,1,0:T(8,128)}, u32[]{:S(2)}) copy-start(f32[2,16,8,128]{3,2,1,0:T(8,128)} %source_hbm.1) | copy-start | bytes 393220

commit v4 on v3

--- a/solution.py
+++ b/solution.py
@@ -16,7 +16,7 @@
 epsilon = 1e-06
 
 
-SIDES = [(dx, dy) for dy in (1, -1, 0) for dx in (0, 1, -1) if (dx, dy) != (0, 0)]
+SIDES = [(1, 1), (1, -1), (-1, 1), (-1, -1), (0, 1), (0, -1), (1, 0), (-1, 0)]
 
 
 def planes(low, high, chunk, body):
@@ -111,7 +111,7 @@
     bc_ref, props_ref, source, sa, sb, ia, inn, ip, ba, bb,
     ga, gb, gn, gp, ea, eb, m, k_own, lap, recip, rhs, z, fold,
     rya, ryb, rx, rca, rcb, g1, g2,
-    local_sem, s1, r1, s2, r2, s3, r3, s4, r4,
+    local_sem, heard, s1, r1, s2, r2, s3, r3, s4, r4,
 ):
     gx, gy = lax.axis_index("gx"), lax.axis_index("gy")
     n_gx, n_gy = lax.axis_size("gx"), lax.axis_size("gy")
@@ -124,6 +124,22 @@
         x = lax.rem(gx + (dx + n_gx), n_gx) if dx else gx
         y = lax.rem(gy + (dy + n_gy), n_gy) if dy else gy
         return x, y
+
+    size1, size2 = n_gx * 4, n_gy // 4
+    me1 = gx * 4 + lax.rem(gy, 4)
+    me2 = lax.div(gy, 4)
+
+    def partner1(step):
+        other = lax.rem(me1 + step, size1)
+        return lax.div(other, 4), me2 * 4 + lax.rem(other, 4)
+
+    def partner2(step):
+        other = lax.rem(me2 + step, size2)
+        return gx, other * 4 + lax.rem(gy, 4)
+
+    barrier = pltpu.get_barrier_semaphore()
+    for dx, dy in SIDES:
+        pl.semaphore_signal(barrier, inc=1, device_id=device(dx, dy), device_id_type=MESH)
 
     loads = [
         pltpu.make_async_copy(storage_hbm, sa.at[:, OWN : OWN + CX], local_sem.at[0]),
@@ -134,33 +150,6 @@
     ]
     for copy in loads:
         copy.start()
-
-    size1, size2 = n_gx * 4, n_gy // 4
-    me1 = gx * 4 + lax.rem(gy, 4)
-    me2 = lax.div(gy, 4)
-
-    def partner1(step):
-        other = lax.rem(me1 + step, size1)
-        return lax.div(other, 4), me2 * 4 + lax.rem(other, 4)
-
-    def partner2(step):
-        other = lax.rem(me2 + step, size2)
-        return gx, other * 4 + lax.rem(gy, 4)
-
-    barrier = pltpu.get_barrier_semaphore()
-    for dx, dy in SIDES:
-        pl.semaphore_signal(barrier, inc=1, device_id=device(dx, dy), device_id_type=MESH)
-
-    def greet(step, carry):
-        pl.semaphore_signal(barrier, inc=1, device_id=partner1(step), device_id_type=MESH)
-        return carry
-
-    def greet2(step, carry):
-        pl.semaphore_signal(barrier, inc=1, device_id=partner2(step), device_id_type=MESH)
-        return carry
-
-    lax.fori_loop(1, size1, greet, 0)
-    lax.fori_loop(1, size2, greet2, 0)
 
     loads[3].wait()
     own_bc = jnp.concatenate(
@@ -176,7 +165,7 @@
         for p in list(range(0, OWN)) + list(range(OWN + CX, EX)):
             rhs[field, p] = zero
 
-    pl.semaphore_wait(barrier, len(SIDES) + size1 - 1 + size2 - 1)
+    pl.semaphore_wait(barrier, len(SIDES))
     loads[1].wait()
 
     first = []
@@ -204,7 +193,7 @@
         push(ba.at[1, half, :], (bb if dy else ba).at[place, half, :], dx, dy)
     n_ids = len(first)
     loads[0].wait()
-    for dx, dy in SIDES:
+    for dx, dy in SIDES[4:6] + SIDES[:4] + SIDES[6:]:
         src_x = {0: slice(5, 21), 1: slice(17, 21), -1: slice(5, 9)}[dx]
         dst_x = {0: slice(5, 21), 1: slice(1, 5), -1: slice(21, 25)}[dx]
         half = {0: slice(0, 8), 1: slice(4, 8), -1: slice(0, 4)}[dy]
@@ -223,6 +212,12 @@
 
     has_n = (gy < n_gy - 1).astype(jnp.float32)
     has_p = (gy > 0).astype(jnp.float32)
+
+    def tell(turn, reach):
+        for way in (reach, -reach):
+            pl.semaphore_signal(
+                heard.at[turn], inc=1, device_id=device(0, way), device_id_type=MESH
+            )
 
     has_w = (gx > 0).astype(jnp.float32)
     has_e = (gx < n_gx - 1).astype(jnp.float32)
@@ -313,7 +308,8 @@
     planes(OWN, OWN + CX, 4, lambda p: [invert(p + i, 0, True) for i in range(4)])
     for copy in first[n_ids:]:
         copy.wait_recv()
-    planes(1, EX - 1, 4, lambda p: [invert(p + i, 1, False) for i in range(4)])
+    tell(0, 2)
+    planes(1, EX - 1, 12, lambda p: [invert(p + i, 1, False) for i in range(12)])
     planes(1, OWN, 4, lambda p: [invert(p + i, 0, False) for i in range(4)])
     planes(OWN + CX, EX - 1, 4, lambda p: [invert(p + i, 0, False) for i in range(4)])
 
@@ -423,7 +419,7 @@
 
         for p in range(4, 9):
             one(p, True, False)
-        planes(9, 17, 4, lambda p: [one(p + i, False, False) for i in range(4)])
+        planes(9, 17, 8, lambda p: [one(p + i, False, False) for i in range(8)])
         for p in range(17, 22):
             one(p, False, True)
 
@@ -465,16 +461,18 @@
             )
 
         def group(index, acc):
-            for i in range(4):
-                acc = one(index * 4 + i, acc)
+            for i in range(8):
+                acc = one(index * 8 + i, acc)
             return acc
 
-        return lax.fori_loop(0, CX // 4, group, (zero, zero, zero))
+        return lax.fori_loop(0, CX // 8, group, (zero, zero, zero))
 
     solve()
     copies = exchange(0, s2, r2)
     for copy in copies:
         copy.wait_recv()
+    pl.semaphore_wait(heard.at[0], 2)
+    tell(1, 4)
     add_up(0)
     dots_a = apply(0)
     for copy in copies:
@@ -483,6 +481,8 @@
     copies = exchange(1, s2, r2)
     for copy in copies:
         copy.wait_recv()
+    pl.semaphore_wait(heard.at[1], 2)
+    tell(2, 8)
     add_up(1)
     dots_b = apply(1)
 
@@ -521,6 +521,7 @@
         return parts[0], copy_of
 
     tile, copy1 = all_sum(tile, g1, me1, size1, partner1, s3, r3)
+    pl.semaphore_wait(heard.at[2], 2)
     tile, copy2 = all_sum(tile, g2, me2, size2, partner2, s4, r4)
     factors = small_problem(total_lanes(jnp.where(rows == lanes, tile, 0.0)), scale)
     table_out = zero
@@ -578,7 +579,7 @@
             buf(2, 2, 2, 2, 5),
             buf(2, 2, 2, 5), buf(2, 2, 2, 4),
             pltpu.VMEM((32, 1, 128), f32), pltpu.VMEM((8, 1, 128), f32),
-            dma((5,)),
+            dma((5,)), pltpu.SemaphoreType.REGULAR((3,)),
             dma((24,)), dma((24,)),
             dma((2, 18)), dma((2, 18)),
             dma((32,)), dma((32,)),

time: 51.1 us -> 49.3 us (0.965)
  Pallas kernels: 49.6 us -> 47.7 us
    pallas_call x1, Pallas kernels: 49.6 us -> 47.7 us  [shards(): pl.pallas_call(functools.partial(kernel, math.sqrt(cells)), out_shape=(ou...]
where the time goes in v4:
time: 49.3 us; the launch traced here: 49.2 us
  Pallas kernels  47.7 us (97%)
  other arithmetic  0.78 us (2%)
  between operations  0.66 us (1%)
    pallas_call x1, Pallas kernels, shards(): pl.pallas_call(functools.partial(kernel, math.sqrt(cells)), out_shape=(ou...  47.7 us

profile of v4, /device:TPU:1, one launch (start us, length us, event | category | flops | bytes accessed | tf_op | source)
XLA Modules:
  0.0 49.2 jit_solution(2069725591533434230)
XLA Ops:
  0.6 0.0 copy-start
  0.6 47.7 %shard_map.76 = (f32[2,16,8,128]{3,2,1,0:T(8,128)S(1)}, f32[2,16,8,128]{3,2,1,0:T(8,128)S(1)}, f32[2,16,8,128]{3,2,1,0:T(8,128)S(1)}, f32[2,16,8,128]{3,2,1,0:T(8,128)S(1)}, f32[8,128]{1,0:T(8,128)S(1)}) custom-call(f32[2,16,8,128]{3,2,1,0:T(8,128)} %source_hbm.1, f32[4,16,8,128]{3,2,1,0:T(8,128)} %storage_hbm.1, s32[16,8,128]{2,1,0:T(8,128)} %ids_hbm.1, ...), custom_call_target="tpu_custom_call" | custom-call | tf_op jit(solution)/shard_map/pallas_call | solution.py:560
  48.4 0.0 copy-done
  48.4 0.8 %multiply_add_fusion = (f32[2,16,8,128]{3,2,1,0:T(8,128)}, f32[2,16,8,128]{3,2,1,0:T(8,128)}, f32[2,16,8,128]{3,2,1,0:T(8,128)}) fusion(f32[2,16,8,128]{3,2,1,0:T(8,128)S(1)} %get-tuple-element.12, f32[2,16,8,128]{3,2,1,0:T(8,128)S(1)} %get-tuple-element.11, f32[2,16,8,128]{3,2,1,0:T(8,128)S(1)} %copy-done, f32[128]{0:T(128)S(1)} %get-tuple-element.16, ...), kind=kLoop, calls=%fused_computation | loop fusion | flops 425984 | bytes 1052672 | tf_op jit(solution)/shard_map/add | solution.py:595
  (1 shorter events, 0.0 us)
Async XLA Ops:
  0.6 47.7 %copy-start = (f32[2,16,8,128]{3,2,1,0:T(8,128)S(1)}, f32[2,16,8,128]{3,2,1,0:T(8,128)}, u32[]{:S(2)}) copy-start(f32[2,16,8,128]{3,2,1,0:T(8,128)} %source_hbm.1) | copy-start | bytes 393220

commit v5 on v4

--- a/solution.py
+++ b/solution.py
@@ -240,11 +240,7 @@
         ea[p] = look(tab_e, id_a)
         eb[p] = jnp.where(rows < 4, look(tab_e, id_n), look(tab_e, id_p))
 
-    def gather_two(p):
-        gather(p)
-        gather(p + 1)
-
-    planes(0, EX, 2, gather_two)
+    planes(0, EX, 13, lambda p: [gather(p + i) for i in range(13)])
 
     loads[2].wait()
 
@@ -304,12 +300,12 @@
             rhs[0, p] = k11 * u + k12 * t
             rhs[1, p] = k21 * u + k22 * t
 
-    planes(1, EX - 1, 2, lambda p: [diagonals(p + i) for i in range(2)])
-    planes(OWN, OWN + CX, 4, lambda p: [invert(p + i, 0, True) for i in range(4)])
+    planes(1, EX - 1, 24, lambda p: [diagonals(p + i) for i in range(24)])
+    planes(OWN, OWN + CX, 8, lambda p: [invert(p + i, 0, True) for i in range(8)])
     for copy in first[n_ids:]:
         copy.wait_recv()
     tell(0, 2)
-    planes(1, EX - 1, 12, lambda p: [invert(p + i, 1, False) for i in range(12)])
+    planes(1, EX - 1, 24, lambda p: [invert(p + i, 1, False) for i in range(24)])
     planes(1, OWN, 4, lambda p: [invert(p + i, 0, False) for i in range(4)])
     planes(OWN + CX, EX - 1, 4, lambda p: [invert(p + i, 0, False) for i in range(4)])
 
@@ -461,11 +457,11 @@
             )
 
         def group(index, acc):
-            for i in range(8):
-                acc = one(index * 8 + i, acc)
+            for i in range(16):
+                acc = one(index * 16 + i, acc)
             return acc
 
-        return lax.fori_loop(0, CX // 8, group, (zero, zero, zero))
+        return lax.fori_loop(0, CX // 16, group, (zero, zero, zero))
 
     solve()
     copies = exchange(0, s2, r2)
@@ -513,7 +509,8 @@
             copy_of(step).wait_recv()
             return carry
 
-        lax.fori_loop(1, size, send, 0)
+        for step in range(1, size):
+            send(step, 0)
         lax.fori_loop(1, size, receive, 0)
         parts = [box[i] for i in range(size)]
         while len(parts) > 1:

time: 49.3 us -> 48.5 us (0.984)
  Pallas kernels: 47.7 us -> 47 us
    pallas_call x1, Pallas kernels: 47.7 us -> 47 us  [shards(): pl.pallas_call(functools.partial(kernel, math.sqrt(cells)), out_shape=(ou...]
where the time goes in v5:
time: 48.5 us; the launch traced here: 48.4 us
  Pallas kernels  47 us (97%)
  other arithmetic  0.78 us (2%)
  between operations  0.66 us (1%)
    pallas_call x1, Pallas kernels, shards(): pl.pallas_call(functools.partial(kernel, math.sqrt(cells)), out_shape=(ou...  47 us

profile of v5, /device:TPU:1, one launch (start us, length us, event | category | flops | bytes accessed | tf_op | source)
XLA Modules:
  0.0 48.4 jit_solution(6071560468729710372)
XLA Ops:
  0.6 0.0 copy-start
  0.6 47.0 %shard_map.76 = (f32[2,16,8,128]{3,2,1,0:T(8,128)S(1)}, f32[2,16,8,128]{3,2,1,0:T(8,128)S(1)}, f32[2,16,8,128]{3,2,1,0:T(8,128)S(1)}, f32[2,16,8,128]{3,2,1,0:T(8,128)S(1)}, f32[8,128]{1,0:T(8,128)S(1)}) custom-call(f32[2,16,8,128]{3,2,1,0:T(8,128)} %source_hbm.1, f32[4,16,8,128]{3,2,1,0:T(8,128)} %storage_hbm.1, s32[16,8,128]{2,1,0:T(8,128)} %ids_hbm.1, ...), custom_call_target="tpu_custom_call" | custom-call | tf_op jit(solution)/shard_map/pallas_call | solution.py:557
  47.6 0.0 copy-done
  47.6 0.8 %multiply_add_fusion = (f32[2,16,8,128]{3,2,1,0:T(8,128)}, f32[2,16,8,128]{3,2,1,0:T(8,128)}, f32[2,16,8,128]{3,2,1,0:T(8,128)}) fusion(f32[2,16,8,128]{3,2,1,0:T(8,128)S(1)} %get-tuple-element.12, f32[2,16,8,128]{3,2,1,0:T(8,128)S(1)} %get-tuple-element.11, f32[2,16,8,128]{3,2,1,0:T(8,128)S(1)} %copy-done, f32[128]{0:T(128)S(1)} %get-tuple-element.16, ...), kind=kLoop, calls=%fused_computation | loop fusion | flops 425984 | bytes 1052672 | tf_op jit(solution)/shard_map/add | solution.py:592
  (1 shorter events, 0.0 us)
Async XLA Ops:
  0.6 47.0 %copy-start = (f32[2,16,8,128]{3,2,1,0:T(8,128)S(1)}, f32[2,16,8,128]{3,2,1,0:T(8,128)}, u32[]{:S(2)}) copy-start(f32[2,16,8,128]{3,2,1,0:T(8,128)} %source_hbm.1) | copy-start | bytes 393220

commit v6 on v5

--- a/solution.py
+++ b/solution.py
@@ -165,8 +165,25 @@
         for p in list(range(0, OWN)) + list(range(OWN + CX, EX)):
             rhs[field, p] = zero
 
+    loads[1].wait()
+    loads[4].wait()
+
+    def table(row):
+        line = jnp.broadcast_to(props_ref[row : row + 1, :], (8, 16))
+        return jnp.concatenate([line, jnp.zeros((8, 112), jnp.float32)], axis=1)
+
+    tab_p, tab_t, tab_e = jnp.sqrt(table(0)), jnp.sqrt(table(1)), table(2)
+
+    def look(tab, ids):
+        return jnp.take_along_axis(tab, ids, axis=1, mode="promise_in_bounds")
+
+    def look_own(p):
+        for f, tab in enumerate((tab_p, tab_t)):
+            ga[f, p] = look(tab, ia[p])
+        ea[p] = look(tab_e, ia[p])
+
+    planes(OWN, OWN + CX, 16, lambda p: [look_own(p + i) for i in range(16)])
     pl.semaphore_wait(barrier, len(SIDES))
-    loads[1].wait()
 
     first = []
 
@@ -199,17 +216,6 @@
         half = {0: slice(0, 8), 1: slice(4, 8), -1: slice(0, 4)}[dy]
         push(sa.at[:, src_x, half, :], (sb if dy else sa).at[:, dst_x, half, :], dx, dy)
 
-    loads[4].wait()
-
-    def table(row):
-        line = jnp.broadcast_to(props_ref[row : row + 1, :], (8, 16))
-        return jnp.concatenate([line, jnp.zeros((8, 112), jnp.float32)], axis=1)
-
-    tab_p, tab_t, tab_e = jnp.sqrt(table(0)), jnp.sqrt(table(1)), table(2)
-
-    def look(tab, ids):
-        return jnp.take_along_axis(tab, ids, axis=1, mode="promise_in_bounds")
-
     has_n = (gy < n_gy - 1).astype(jnp.float32)
     has_p = (gy > 0).astype(jnp.float32)
 
@@ -229,18 +235,24 @@
     def gather(p):
         inside = ((p >= OWN) | (gx > 0)) & ((p < OWN + CX) | (gx < n_gx - 1))
         inside = inside.astype(jnp.float32)
-        id_a, id_n, id_p = ia[p], inn[p], ip[p]
+        id_n, id_p = inn[p], ip[p]
         for f, tab in enumerate((tab_p, tab_t)):
-            ga[f, p] = look(tab, id_a) * inside
             n_tile = look(tab, id_n) * (inside * has_n)
             p_tile = look(tab, id_p) * (inside * has_p)
             gn[f, p] = n_tile
             gp[f, p] = p_tile
             gb[f, p] = jnp.where(rows < 4, n_tile, p_tile)
-        ea[p] = look(tab_e, id_a)
         eb[p] = jnp.where(rows < 4, look(tab_e, id_n), look(tab_e, id_p))
 
-    planes(0, EX, 13, lambda p: [gather(p + i) for i in range(13)])
+    def look_beside(p, inside):
+        for f, tab in enumerate((tab_p, tab_t)):
+            ga[f, p] = look(tab, ia[p]) * inside
+        ea[p] = look(tab_e, ia[p])
+
+    for p in range(OWN):
+        look_beside(p, has_w)
+        look_beside(p + OWN + CX, has_e)
+    planes(0, EX, 26, lambda p: [gather(p + i) for i in range(26)])
 
     loads[2].wait()
 
@@ -511,7 +523,8 @@
 
         for step in range(1, size):
             send(step, 0)
-        lax.fori_loop(1, size, receive, 0)
+        for step in range(1, size):
+            receive(step, 0)
         parts = [box[i] for i in range(size)]
         while len(parts) > 1:
             parts = [parts[i] + parts[i + 1] for i in range(0, len(parts), 2)]

time: 48.5 us -> 48.4 us (level)
  no operation moved by 1% of the time
where the time goes in v6:
time: 48.4 us; the launch traced here: 48.3 us
  Pallas kernels  46.9 us (97%)
  other arithmetic  0.78 us (2%)
  between operations  0.66 us (1%)
    pallas_call x1, Pallas kernels, shards(): pl.pallas_call(functools.partial(kernel, math.sqrt(cells)), out_shape=(ou...  46.9 us

profile of v6, /device:TPU:1, one launch (start us, length us, event | category | flops | bytes accessed | tf_op | source)
XLA Modules:
  0.0 48.3 jit_solution(8460129518132717251)
XLA Ops:
  0.6 0.0 copy-start
  0.6 46.9 %shard_map.76 = (f32[2,16,8,128]{3,2,1,0:T(8,128)S(1)}, f32[2,16,8,128]{3,2,1,0:T(8,128)S(1)}, f32[2,16,8,128]{3,2,1,0:T(8,128)S(1)}, f32[2,16,8,128]{3,2,1,0:T(8,128)S(1)}, f32[8,128]{1,0:T(8,128)S(1)}) custom-call(f32[2,16,8,128]{3,2,1,0:T(8,128)} %source_hbm.1, f32[4,16,8,128]{3,2,1,0:T(8,128)} %storage_hbm.1, s32[16,8,128]{2,1,0:T(8,128)} %ids_hbm.1, ...), custom_call_target="tpu_custom_call" | custom-call | tf_op jit(solution)/shard_map/pallas_call | solution.py:570
  47.5 0.0 copy-done
  47.5 0.8 %multiply_add_fusion = (f32[2,16,8,128]{3,2,1,0:T(8,128)}, f32[2,16,8,128]{3,2,1,0:T(8,128)}, f32[2,16,8,128]{3,2,1,0:T(8,128)}) fusion(f32[2,16,8,128]{3,2,1,0:T(8,128)S(1)} %get-tuple-element.12, f32[2,16,8,128]{3,2,1,0:T(8,128)S(1)} %get-tuple-element.11, f32[2,16,8,128]{3,2,1,0:T(8,128)S(1)} %copy-done, f32[128]{0:T(128)S(1)} %get-tuple-element.16, ...), kind=kLoop, calls=%fused_computation | loop fusion | flops 425984 | bytes 1052672 | tf_op jit(solution)/shard_map/add | solution.py:605
  (1 shorter events, 0.0 us)
Async XLA Ops:
  0.6 46.9 %copy-start = (f32[2,16,8,128]{3,2,1,0:T(8,128)S(1)}, f32[2,16,8,128]{3,2,1,0:T(8,128)}, u32[]{:S(2)}) copy-start(f32[2,16,8,128]{3,2,1,0:T(8,128)} %source_hbm.1) | copy-start | bytes 393220

commit v7 on v6

--- a/solution.py
+++ b/solution.py
@@ -551,8 +551,10 @@
         copy.wait_send()
     for copy in copies:
         copy.wait_send()
-    lax.fori_loop(1, size1, drain1, 0)
-    lax.fori_loop(1, size2, drain2, 0)
+    for step in range(1, size1):
+        drain1(step, 0)
+    for step in range(1, size2):
+        drain2(step, 0)
 
 
 def shards(adjoint_source, storage, soil_ids, bc_mask, soil_props):

time: 48.4 us -> 48.2 us (level)
  no operation moved by 1% of the time
where the time goes in v7:
time: 48.2 us; the launch traced here: 48.1 us
  Pallas kernels  46.7 us (97%)
  other arithmetic  0.78 us (2%)
  between operations  0.66 us (1%)
    pallas_call x1, Pallas kernels, shards(): pl.pallas_call(functools.partial(kernel, math.sqrt(cells)), out_shape=(ou...  46.7 us

profile of v7, /device:TPU:1, one launch (start us, length us, event | category | flops | bytes accessed | tf_op | source)
XLA Modules:
  0.0 48.1 jit_solution(8948369986015591968)
XLA Ops:
  0.6 0.0 copy-start
  0.6 46.7 %shard_map.76 = (f32[2,16,8,128]{3,2,1,0:T(8,128)S(1)}, f32[2,16,8,128]{3,2,1,0:T(8,128)S(1)}, f32[2,16,8,128]{3,2,1,0:T(8,128)S(1)}, f32[2,16,8,128]{3,2,1,0:T(8,128)S(1)}, f32[8,128]{1,0:T(8,128)S(1)}) custom-call(f32[2,16,8,128]{3,2,1,0:T(8,128)} %source_hbm.1, f32[4,16,8,128]{3,2,1,0:T(8,128)} %storage_hbm.1, s32[16,8,128]{2,1,0:T(8,128)} %ids_hbm.1, ...), custom_call_target="tpu_custom_call" | custom-call | tf_op jit(solution)/shard_map/pallas_call | solution.py:572
  47.4 0.0 copy-done
  47.4 0.8 %multiply_add_fusion = (f32[2,16,8,128]{3,2,1,0:T(8,128)}, f32[2,16,8,128]{3,2,1,0:T(8,128)}, f32[2,16,8,128]{3,2,1,0:T(8,128)}) fusion(f32[2,16,8,128]{3,2,1,0:T(8,128)S(1)} %get-tuple-element.12, f32[2,16,8,128]{3,2,1,0:T(8,128)S(1)} %get-tuple-element.11, f32[2,16,8,128]{3,2,1,0:T(8,128)S(1)} %copy-done, f32[128]{0:T(128)S(1)} %get-tuple-element.16, ...), kind=kLoop, calls=%fused_computation | loop fusion | flops 425984 | bytes 1052672 | tf_op jit(solution)/shard_map/add | solution.py:607
  (1 shorter events, 0.0 us)
Async XLA Ops:
  0.6 46.7 %copy-start = (f32[2,16,8,128]{3,2,1,0:T(8,128)S(1)}, f32[2,16,8,128]{3,2,1,0:T(8,128)}, u32[]{:S(2)}) copy-start(f32[2,16,8,128]{3,2,1,0:T(8,128)} %source_hbm.1) | copy-start | bytes 393220
